TPU v7x, 256 devices: a whole 4x4x8 slice. The times are simulated.
256 devices in a mesh: row: 16 (over x_hi, y, core), col: 16 (over z, x_lo).
Axes of the slice: x: 4 (x_hi: 2, x_lo: 2; x = x_hi * 2 + x_lo), y: 4, z: 8, core: 2. Of those that a mesh axis runs over, the one named last changes fastest.
Arguments:
- object_field: float32 [2, 2, 2048, 2048], P(None, None, 'row', 'col'), may hold values from -6 to 6
- probe_field: float32 [2, 128, 128], replicated, may hold values from -6 to 6
- intensity: float32 [16, 16, 6, 128, 128], P('row', 'col'), may hold values from 0.25 to 4
- counts: int32 [16, 16], P('row', 'col'), may hold values from 2 to 6, as said below
- offsets: int32 [16, 16, 6, 2], P('row', 'col'), may hold values from 0 to 64, as said below
Outputs:
- updated_object: float32 [2, 2, 2048, 2048], P(None, None, 'row', 'col')
Inputs may be any that keep to these rules, and one draw needn't show every extreme that they name: `counts`: each tile has at least 2 and at most 6 live slots; some tile has exactly 6 and some exactly 2. `offsets`: offsets keep every window inside its bordered tile; both ends of the range occur in every draw.
All inputs are finite; a program needn't handle non-finite values.
Results may differ from a plain program's by a relative error of at most 0.0003.
Values sent between devices are 32-bit elements; how exact they have to be, the bound alone decides.
No kernel may reach another device: no remote copies, remote signals or barrier semaphores. Data moves between devices by JAX's collectives and lax.ppermute only.
A program may use at most 64 MiB of HBM per device.

v0:
```python
import functools

import jax
import jax.numpy as jnp
import numpy as np
from jax import lax
from jax.experimental import pallas as pl
from jax.experimental.pallas import tpu as pltpu
from jax.sharding import PartitionSpec as P

BORDER = 32
LANES = 128
step_size = 0.25
chirp = 0.7


def tables(size):
    index = np.arange(size)
    angles = -2.0 * np.pi / size * (index[:, None] * index[None, :] % size)
    fourier = np.exp(1j * angles) / np.sqrt(size)
    frequency = np.where(index < size // 2, index, index - size)
    kernel = np.exp(-1j * chirp * np.pi / size * frequency * frequency)
    propagator = fourier.conj() @ (kernel[:, None] * fourier)

    def block(matrix):
        return np.block([[matrix.real, matrix.imag], [-matrix.imag, matrix.real]])

    blocks = np.stack(
        [
            block(propagator.T),
            block(propagator.conj()),
            block(fourier),
            block(fourier.conj()),
        ]
    ).astype(np.float32)
    high = blocks.astype(jnp.bfloat16)
    low = (blocks - high.astype(np.float32)).astype(jnp.bfloat16)
    return jnp.asarray(np.stack([high, low], axis=1))


PT, PC, FF, FC = range(4)


def lane_iota(rows):
    return lax.broadcasted_iota(jnp.int32, (rows, LANES), 1)


def split(value):
    high = value.astype(jnp.bfloat16)
    low = (value - high.astype(jnp.float32)).astype(jnp.bfloat16)
    return high, low


def pack_quarter(planes, first):
    lane = lane_iota(planes[0].shape[0])
    packed = None
    for p in range(4):
        shift = (32 * p - first) % LANES
        moved = planes[p] if shift == 0 else pltpu.roll(planes[p], shift, 1)
        packed = moved if p == 0 else jnp.where(lane >= 32 * p, moved, packed)
    return packed


def unpack_quarter(packed, p, first):
    shift = (first - 32 * p) % LANES
    return packed if shift == 0 else pltpu.roll(packed, shift, 1)


def pack_half(low, high):
    lane = lane_iota(low.shape[0])
    inner = (lane >= 32) & (lane < 96)
    return jnp.where(inner, pltpu.roll(high, 64, 1), low)


def outer(lane, low_part, high_part):
    zero = jnp.zeros_like(low_part)
    return jnp.where(lane < 32, low_part, jnp.where(lane >= 96, high_part, zero))


def edges():
    row = lax.axis_index("row")
    col = lax.axis_index("col")
    rows = lax.axis_size("row")
    cols = lax.axis_size("col")
    return row > 0, row < rows - 1, col > 0, col < cols - 1


def halo_pack_kernel(core_ref, above_ref, below_ref, left_ref, right_ref):
    has_up, has_down, _, _ = edges()
    parts = (
        (0, 32, above_ref, 0, has_up),
        (32, 128, core_ref, 0, None),
        (160, 32, below_ref, 0, has_down),
    )
    for start, length, ref, at, flag in parts:
        planes = [ref[p, pl.ds(at, length), :] for p in range(4)]
        if flag is not None:
            planes = [jnp.where(flag, plane, 0.0) for plane in planes]
        left_ref[pl.ds(start, length), :] = pack_quarter(planes, 0)
        right_ref[pl.ds(start, length), :] = pack_quarter(planes, 96)


def gradients(b_ref, probe_ref, intensity_ref, live, offsets_ref, w_ref, g_ref, scratch):
    win_ref, prop_ref, xh_ref, xl_ref, zh_ref, zl_ref = scratch
    slots = intensity_ref.shape[0]
    size = intensity_ref.shape[1]
    lane = lane_iota(size)
    rows_at, shifts, first_masks = [], [], []
    for s in range(slots):
        column = offsets_ref[s, 1]
        shift = lax.rem(column + 96, LANES)
        rows_at.append(offsets_ref[s, 0])
        shifts.append(shift)
        ahead = jnp.where(lane >= shift, 1, 0)
        wrapped = jnp.where(column < 32, 1, 0)
        first_masks.append(ahead != wrapped)

    g_ref[...] = jnp.zeros_like(g_ref)

    def put_x(s, real, imag):
        at = pl.ds(size * s, size)
        for half, value in ((0, real), (1, imag)):
            high, low = split(value)
            xh_ref[at, pl.ds(LANES * half, LANES)] = high
            xl_ref[at, pl.ds(LANES * half, LANES)] = low

    def right(m):
        high, low = w_ref[m, 0], w_ref[m, 1]
        table = jnp.concatenate([high, high, low], axis=0)
        for pair in range(slots // 2):
            at = pl.ds(2 * size * pair, 2 * size)
            xh = xh_ref[at, :]
            xl = xl_ref[at, :]
            y = jnp.dot(
                jnp.concatenate([xh, xl, xh], axis=1),
                table,
                preferred_element_type=jnp.float32,
            )
            for q in range(2):
                s = 2 * pair + q
                for half in range(2):
                    part = y[size * q : size * (q + 1), LANES * half : LANES * (half + 1)]
                    part_high, part_low = split(part)
                    where_at = (pl.ds(size * half, size), pl.ds(size * s, size))
                    zh_ref[where_at] = part_high
                    zl_ref[where_at] = part_low

    def left(m, post):
        high, low = w_ref[m, 0], w_ref[m, 1]
        table = jnp.concatenate([high, low, high], axis=1)
        for pair in range(slots // 2):
            at = pl.ds(2 * size * pair, 2 * size)
            zh = zh_ref[:, at]
            zl = zl_ref[:, at]
            y = jnp.dot(
                table,
                jnp.concatenate([zh, zh, zl], axis=0),
                preferred_element_type=jnp.float32,
            )
            for q in range(2):
                post(
                    2 * pair + q,
                    y[:size, size * q : size * (q + 1)],
                    y[size:, size * q : size * (q + 1)],
                )

    def accumulate(s, plane, value):
        moved = pltpu.roll(value, shifts[s], 1)
        is_live = s < live
        moved = jnp.where(is_live, moved, 0.0)
        at = pl.ds(rows_at[s], size)
        zero = jnp.zeros_like(moved)
        g_ref[0, plane, at, :] += jnp.where(first_masks[s], moved, zero)
        g_ref[1, plane, at, :] += jnp.where(first_masks[s], zero, moved)

    for s in range(slots):
        at = pl.ds(rows_at[s], size)
        back = lax.rem(LANES - shifts[s], LANES)
        for p in range(4):
            mixed = jnp.where(first_masks[s], b_ref[0, p, at, :], b_ref[1, p, at, :])
            win_ref[p, s] = pltpu.roll(mixed, back, 1)
        probe_real, probe_imag = probe_ref[0], probe_ref[1]
        a_real, a_imag = win_ref[0, s], win_ref[1, s]
        put_x(
            s,
            probe_real * a_real - probe_imag * a_imag,
            probe_real * a_imag + probe_imag * a_real,
        )

    def after_propagation(s, real, imag):
        prop_ref[s, 0] = real
        prop_ref[s, 1] = imag
        a_real, a_imag = win_ref[2, s], win_ref[3, s]
        put_x(s, real * a_real - imag * a_imag, real * a_imag + imag * a_real)

    def after_far(s, real, imag):
        measured = intensity_ref[s]
        amplitude = measured * lax.rsqrt(measured)
        ratio = amplitude * lax.rsqrt(real * real + imag * imag + 1.0)
        scale = 1.0 - ratio
        put_x(s, real * scale, imag * scale)

    def after_back(s, real, imag):
        prop_real, prop_imag = prop_ref[s, 0], prop_ref[s, 1]
        accumulate(s, 2, prop_real * real + prop_imag * imag)
        accumulate(s, 3, prop_real * imag - prop_imag * real)
        a_real, a_imag = win_ref[2, s], win_ref[3, s]
        put_x(s, a_real * real + a_imag * imag, a_real * imag - a_imag * real)

    def after_last(s, real, imag):
        probe_real, probe_imag = probe_ref[0], probe_ref[1]
        accumulate(s, 0, probe_real * real + probe_imag * imag)
        accumulate(s, 1, probe_real * imag - probe_imag * real)

    right(PT)
    left(PC, after_propagation)
    right(FF)
    left(FC, after_far)
    right(FC)
    left(FF, after_back)
    right(PC)
    left(PT, after_last)


def row_pack(g_ref, start, length, out_ref):
    at = pl.ds(start, length)
    for p in range(4):
        out_ref[p] = g_ref[0, p, at, :]
    for p in range(2):
        out_ref[4 + p] = pack_half(g_ref[1, p, at, :], g_ref[1, p + 2, at, :])


def row_unpack(ref, tile, p):
    if tile == 0:
        return ref[p]
    packed = ref[4 + p % 2]
    return packed if p < 2 else pltpu.roll(packed, 64, 1)


def first_kernel(
    core_ref, above_ref, below_ref, from_left_ref, from_right_ref,
    probe_ref, intensity_ref, counts_ref, offsets_ref, w_ref,
    b_ref, g_ref, up_ref, down_ref, *scratch,
):
    has_up, has_down, has_left, has_right = edges()
    rows = b_ref.shape[2]
    lane = lane_iota(rows)
    for p in range(4):
        b_ref[0, p, pl.ds(0, 32), :] = jnp.where(has_up, above_ref[p], 0.0)
        b_ref[0, p, pl.ds(32, 128), :] = core_ref[p]
        b_ref[0, p, pl.ds(160, 32), :] = jnp.where(has_down, below_ref[p], 0.0)
        from_right = jnp.where(has_right, from_right_ref[...], 0.0)
        from_left = jnp.where(has_left, from_left_ref[...], 0.0)
        b_ref[1, p] = outer(
            lane, unpack_quarter(from_right, p, 0), unpack_quarter(from_left, p, 96)
        )
    gradients(
        b_ref, probe_ref, intensity_ref, counts_ref[0, 0], offsets_ref, w_ref, g_ref, scratch
    )
    row_pack(g_ref, 0, 64, up_ref)
    row_pack(g_ref, 128, 64, down_ref)


def first_sum_kernel(g_ref, from_up_ref, from_down_ref, sum_ref, left_ref, right_ref):
    has_up, has_down, _, _ = edges()
    rows = sum_ref.shape[2]
    lane = lane_iota(rows)
    for t in range(2):
        for p in range(4):
            top = jnp.where(has_up, row_unpack(from_up_ref, t, p), 0.0)
            bottom = jnp.where(has_down, row_unpack(from_down_ref, t, p), 0.0)
            sum_ref[t, p, pl.ds(0, 64), :] = g_ref[t, p, pl.ds(0, 64), :] + top
            sum_ref[t, p, pl.ds(64, 64), :] = g_ref[t, p, pl.ds(64, 64), :]
            sum_ref[t, p, pl.ds(128, 64), :] = g_ref[t, p, pl.ds(128, 64), :] + bottom
    for p in range(2):
        to_right, to_left = [], []
        for q in (p, p + 2):
            near, far = sum_ref[0, q], sum_ref[1, q]
            to_right.append(jnp.where(lane < 32, far, near))
            to_left.append(jnp.where(lane < 32, near, far))
        right_ref[p] = pack_half(*to_right)
        left_ref[p] = pack_half(*to_left)


def second_kernel(
    b_ref, sum_ref, from_left_ref, from_right_ref,
    probe_ref, intensity_ref, counts_ref, offsets_ref, w_ref,
    core_ref, g_ref, up_ref, down_ref, new_ref, *scratch,
):
    has_up, has_down, has_left, has_right = edges()
    rows = b_ref.shape[2]
    lane = lane_iota(rows)
    row = lax.broadcasted_iota(jnp.int32, (rows, LANES), 0)
    first_row = jnp.where(has_up, 0, 32)
    last_row = jnp.where(has_down, rows, rows - 32)
    inside = (row >= first_row) & (row < last_row)
    low_limit = jnp.where(has_right, 32, 0)
    high_limit = jnp.where(has_left, 96, LANES)
    inside_far = inside & ((lane < low_limit) | (lane >= high_limit))
    for p in range(4):
        left = jnp.where(has_left, from_left_ref[p % 2], 0.0)
        right = jnp.where(has_right, from_right_ref[p % 2], 0.0)
        if p >= 2:
            left = pltpu.roll(left, 64, 1)
            right = pltpu.roll(right, 64, 1)
        near = b_ref[0, p] - step_size * (sum_ref[0, p] + outer(lane, left, right))
        far = b_ref[1, p] - step_size * (sum_ref[1, p] + outer(lane, right, left))
        near = jnp.where(inside, near, 0.0)
        new_ref[0, p] = near
        new_ref[1, p] = jnp.where(inside_far, far, 0.0)
        core_ref[p] = near[32:160]
    gradients(
        new_ref, probe_ref, intensity_ref, counts_ref[0, 0], offsets_ref, w_ref, g_ref, scratch
    )
    row_pack(g_ref, 0, 32, up_ref)
    row_pack(g_ref, 160, 32, down_ref)


def second_sum_kernel(
    core_ref, g_ref, from_up_ref, from_down_ref, out_ref, left_ref, right_ref
):
    has_up, has_down, _, _ = edges()
    for start, length in ((0, 32), (32, 64), (96, 32)):
        far = []
        for t in range(2):
            for p in range(4):
                value = g_ref[t, p, pl.ds(32 + start, length), :]
                if start == 0:
                    value = value + jnp.where(has_up, row_unpack(from_up_ref, t, p), 0.0)
                if start == 96:
                    value = value + jnp.where(has_down, row_unpack(from_down_ref, t, p), 0.0)
                if t == 0:
                    at = pl.ds(start, length)
                    out_ref[p, at, :] = core_ref[p, at, :] - step_size * value
                else:
                    far.append(value)
        right_ref[pl.ds(start, length), :] = pack_quarter(far, 0)
        left_ref[pl.ds(start, length), :] = pack_quarter(far, 96)


def final_kernel(core_ref, from_left_ref, from_right_ref, out_ref):
    _, _, has_left, has_right = edges()
    lane = lane_iota(core_ref.shape[1])
    left = jnp.where(has_left, from_left_ref[...], 0.0)
    right = jnp.where(has_right, from_right_ref[...], 0.0)
    for p in range(4):
        added = outer(lane, unpack_quarter(left, p, 0), unpack_quarter(right, p, 96))
        out_ref[p] = core_ref[p] - step_size * added


VMEM = pl.BlockSpec(memory_space=pltpu.VMEM)
SMEM = pl.BlockSpec(memory_space=pltpu.SMEM)


def call(kernel, outs, specs, limit, scratch=()):
    shapes = [jax.ShapeDtypeStruct(shape, jnp.float32) for shape in outs]
    return pl.pallas_call(
        kernel,
        out_shape=shapes,
        in_specs=specs,
        out_specs=[VMEM] * len(outs),
        scratch_shapes=list(scratch),
        compiler_params=pltpu.CompilerParams(vmem_limit_bytes=limit << 20),
    )


def shifted(value, axis, by):
    count = lax.axis_size(axis)
    return lax.ppermute(value, axis, [(i, (i + by) % count) for i in range(count)])


def exchange(axis, to_low, to_high):
    from_low = shifted(to_high, axis, 1)
    from_high = shifted(to_low, axis, -1)
    return from_low, from_high


def local(object_field, probe_field, intensity, counts, offsets):
    size = object_field.shape[-1]
    slots = intensity.shape[2]
    tall = size + 2 * BORDER
    weights = tables(size)
    core = object_field.reshape(4, size, size)
    own_intensity = intensity[0, 0]
    own_offsets = offsets[0, 0]
    common = (probe_field, own_intensity, counts, own_offsets, weights)
    common_specs = [VMEM, VMEM, SMEM, SMEM, VMEM]
    scratch = (
        pltpu.VMEM((4, slots, size, size), jnp.float32),
        pltpu.VMEM((slots, 2, size, size), jnp.float32),
        pltpu.VMEM((slots * size, 2 * size), jnp.bfloat16),
        pltpu.VMEM((slots * size, 2 * size), jnp.bfloat16),
        pltpu.VMEM((2 * size, slots * size), jnp.bfloat16),
        pltpu.VMEM((2 * size, slots * size), jnp.bfloat16),
    )
    full = (2, 4, tall, size)

    above, below = exchange("row", core[:, :BORDER], core[:, size - BORDER :])
    to_left, to_right = call(
        halo_pack_kernel, [(tall, LANES)] * 2, [VMEM] * 3, 8
    )(core, above, below)
    left, right = exchange("col", to_left, to_right)
    bordered, grads, up, down = call(
        first_kernel,
        [full, full, (6, 64, size), (6, 64, size)],
        [VMEM] * 5 + common_specs,
        32,
        scratch,
    )(core, above, below, left, right, *common)
    from_up, from_down = exchange("row", up, down)
    summed, to_left, to_right = call(
        first_sum_kernel, [full, (2, tall, size), (2, tall, size)], [VMEM] * 3, 16
    )(grads, from_up, from_down)
    left, right = exchange("col", to_left, to_right)
    core, grads, up, down = call(
        second_kernel,
        [(4, size, size), full, (6, 32, size), (6, 32, size)],
        [VMEM] * 4 + common_specs,
        32,
        (pltpu.VMEM(full, jnp.float32),) + scratch,
    )(bordered, summed, left, right, *common)
    from_up, from_down = exchange("row", up, down)
    core, to_left, to_right = call(
        second_sum_kernel,
        [(4, size, size), (size, LANES), (size, LANES)],
        [VMEM] * 4,
        16,
    )(core, grads, from_up, from_down)
    left, right = exchange("col", to_left, to_right)
    (result,) = call(final_kernel, [(4, size, size)], [VMEM] * 3, 8)(core, left, right)
    return result.reshape(2, 2, size, size)


def solution(mesh):
    in_specs = (
        P(None, None, "row", "col"),
        P(),
        P("row", "col", None, None, None),
        P("row", "col"),
        P("row", "col", None, None),
    )
    out_specs = P(None, None, "row", "col")
    return jax.shard_map(local, mesh=mesh, in_specs=in_specs, out_specs=out_specs, check_vma=False)
```

profile of v0, /device:TPU:123, one launch (start us, length us, event | category | flops | bytes accessed | tf_op | source)
XLA Modules:
  0.0 69.6 jit_solution(12461896340696466545)
XLA Ops:
  0.0 0.0 copy-start.2
  0.0 0.0 copy-start.3
  0.0 0.9 %fusion = (f32[4,32,128]{2,1,0:T(8,128)S(1)}, f32[4,32,128]{2,1,0:T(8,128)S(1)}) fusion(f32[4,128,128]{2,1,0:T(8,128)} %bitcast.4), kind=kLoop, calls=%fused_computation | loop fusion | bytes 262144 | tf_op jit(solution)/shard_map/slice | solution.py:398
  1.0 0.8 %collective-permute-start.1 = (f32[4,32,128]{2,1,0:T(8,128)S(1)}, f32[4,32,128]{2,1,0:T(8,128)S(1)}, u32[]{:S(2)}, u32[]{:S(2)}) collective-permute-start(f32[4,32,128]{2,1,0:T(8,128)S(1)} %get-tuple-element.37), channel_id=1, source_target_pairs={{0,240},{16,0},{32,16},{48,32},{64,48},{80,64},{96,80},{112,96},{1... | collective-permute-start | bytes 196616 | tf_op jit(solution)/shard_map/ppermute | solution.py:369
  1.7 4.7 %collective-permute-start = (f32[4,32,128]{2,1,0:T(8,128)S(1)}, f32[4,32,128]{2,1,0:T(8,128)S(1)}, u32[]{:S(2)}, u32[]{:S(2)}) collective-permute-start(f32[4,32,128]{2,1,0:T(8,128)S(1)} %get-tuple-element.38), channel_id=1, source_target_pairs={{0,16},{16,32},{32,48},{48,64},{64,80},{80,96},{96,112},{112,128},... | collective-permute-start | bytes 196616 | tf_op jit(solution)/shard_map/ppermute | solution.py:369
  6.4 1.9 %collective-permute-done.1.below_ref = f32[4,32,128]{2,1,0:T(8,128)S(1)} collective-permute-done((f32[4,32,128]{2,1,0:T(8,128)S(1)}, f32[4,32,128]{2,1,0:T(8,128)S(1)}, u32[]{:S(2)}, u32[]{:S(2)}) %collective-permute-start.1) | collective-permute-done | bytes 65568 | tf_op jit(solution)/shard_map/ppermute | solution.py:369
  8.3 0.0 collective-permute-done.above_ref
  8.3 0.0 copy-done.2
  8.3 0.2 shard_map.64
  8.6 2.9 %collective-permute-start.2 = (f32[192,128]{1,0:T(8,128)S(1)}, f32[192,128]{1,0:T(8,128)S(1)}, u32[]{:S(2)}, u32[]{:S(2)}) collective-permute-start(f32[192,128]{1,0:T(8,128)S(1)} %get-tuple-element.21), channel_id=1, source_target_pairs={{0,1},{1,2},{2,3},{3,4},{4,5},{5,6},{6,7},{7,8},{8,9},{9,10},{10,1... | collective-permute-start | bytes 294920 | tf_op jit(solution)/shard_map/ppermute | solution.py:369
  11.5 0.0 collective-permute-start.3
  12.1 0.0 copy-start.5
  12.1 0.7 copy-done.5
  12.8 0.1 copy.7.offsets_ref
  12.9 0.2 collective-permute-done.2.from_left_ref
  13.1 3.9 %collective-permute-done.3.from_right_ref = f32[192,128]{1,0:T(8,128)S(1)} collective-permute-done((f32[192,128]{1,0:T(8,128)S(1)}, f32[192,128]{1,0:T(8,128)S(1)}, u32[]{:S(2)}, u32[]{:S(2)}) %collective-permute-start.3) | collective-permute-done | bytes 98336 | tf_op jit(solution)/shard_map/ppermute | solution.py:369
  17.1 0.0 copy-done.3
  17.1 0.0 copy-start
  17.1 1.2 %copy-done = bf16[4,2,256,256]{3,2,1,0:T(8,128)(2,1)S(1)} copy-done((bf16[4,2,256,256]{3,2,1,0:T(8,128)(2,1)S(1)}, bf16[4,2,256,256]{3,2,1,0:T(8,128)(2,1)}, u32[]{:S(2)}) %copy-start) | copy-done | bytes 1048600
  18.3 0.0 copy-start.4
  18.3 0.9 %copy-done.4 = f32[2,128,128]{2,1,0:T(8,128)S(1)} copy-done((f32[2,128,128]{2,1,0:T(8,128)S(1)}, f32[2,128,128]{2,1,0:T(8,128)}, u32[]{:S(2)}) %copy-start.4) | copy-done | bytes 131096
  19.2 4.9 %shard_map.65 = (f32[2,4,192,128]{3,2,1,0:T(8,128)S(1)}, f32[2,4,192,128]{3,2,1,0:T(8,128)S(1)}, f32[6,64,128]{2,1,0:T(8,128)S(1)}, f32[6,64,128]{2,1,0:T(8,128)S(1)}) custom-call(f32[4,128,128]{2,1,0:T(8,128)S(1)} %bitcast.6, f32[4,32,128]{2,1,0:T(8,128)S(1)} %collective-permute-done.above_ref, f32[4,32,128]{2,1,0:T(8,128)S(1)} %collective-permute-done.1.below_ref, ...), custom_call_target="tpu_custom_call" | custom-call | tf_op jit(solution)/shard_map/pallas_call | solution.py:403
  24.1 0.0 copy-start.1
  24.1 6.3 %collective-permute-start.4 = (f32[6,64,128]{2,1,0:T(8,128)S(1)}, f32[6,64,128]{2,1,0:T(8,128)S(1)}, u32[]{:S(2)}, u32[]{:S(2)}) collective-permute-start(f32[6,64,128]{2,1,0:T(8,128)S(1)} %get-tuple-element.25), channel_id=1, source_target_pairs={{0,16},{16,32},{32,48},{48,64},{64,80},{80,96},{96,112},{112,128},... | collective-permute-start | bytes 589832 | tf_op jit(solution)/shard_map/ppermute | solution.py:369
  30.4 0.0 collective-permute-start.5
  30.4 5.0 %collective-permute-done.4.from_up_ref = f32[6,64,128]{2,1,0:T(8,128)S(1)} collective-permute-done((f32[6,64,128]{2,1,0:T(8,128)S(1)}, f32[6,64,128]{2,1,0:T(8,128)S(1)}, u32[]{:S(2)}, u32[]{:S(2)}) %collective-permute-start.4) | collective-permute-done | bytes 196640 | tf_op jit(solution)/shard_map/ppermute | solution.py:369
  35.3 3.7 %collective-permute-done.5.from_down_ref = f32[6,64,128]{2,1,0:T(8,128)S(1)} collective-permute-done((f32[6,64,128]{2,1,0:T(8,128)S(1)}, f32[6,64,128]{2,1,0:T(8,128)S(1)}, u32[]{:S(2)}, u32[]{:S(2)}) %collective-permute-start.5) | collective-permute-done | bytes 196640 | tf_op jit(solution)/shard_map/ppermute | solution.py:369
  39.1 0.2 shard_map.66
  39.3 1.6 %collective-permute-start.6 = (f32[2,192,128]{2,1,0:T(8,128)S(1)}, f32[2,192,128]{2,1,0:T(8,128)S(1)}, u32[]{:S(2)}, u32[]{:S(2)}) collective-permute-start(f32[2,192,128]{2,1,0:T(8,128)S(1)} %get-tuple-element.28), channel_id=1, source_target_pairs={{0,1},{1,2},{2,3},{3,4},{4,5},{5,6},{6,7},{7,8},{8,9},{9,10},{10,1... | collective-permute-start | bytes 589832 | tf_op jit(solution)/shard_map/ppermute | solution.py:369
  40.9 1.0 %collective-permute-start.7 = (f32[2,192,128]{2,1,0:T(8,128)S(1)}, f32[2,192,128]{2,1,0:T(8,128)S(1)}, u32[]{:S(2)}, u32[]{:S(2)}) collective-permute-start(f32[2,192,128]{2,1,0:T(8,128)S(1)} %get-tuple-element.29), channel_id=1, source_target_pairs={{0,15},{1,0},{2,1},{3,2},{4,3},{5,4},{6,5},{7,6},{8,7},{9,8},{10,9... | collective-permute-start | bytes 589832 | tf_op jit(solution)/shard_map/ppermute | solution.py:369
  41.9 2.8 %collective-permute-done.6.from_left_ref = f32[2,192,128]{2,1,0:T(8,128)S(1)} collective-permute-done((f32[2,192,128]{2,1,0:T(8,128)S(1)}, f32[2,192,128]{2,1,0:T(8,128)S(1)}, u32[]{:S(2)}, u32[]{:S(2)}) %collective-permute-start.6) | collective-permute-done | bytes 196640 | tf_op jit(solution)/shard_map/ppermute | solution.py:369
  44.7 2.8 %collective-permute-done.7.from_right_ref = f32[2,192,128]{2,1,0:T(8,128)S(1)} collective-permute-done((f32[2,192,128]{2,1,0:T(8,128)S(1)}, f32[2,192,128]{2,1,0:T(8,128)S(1)}, u32[]{:S(2)}, u32[]{:S(2)}) %collective-permute-start.7) | collective-permute-done | bytes 196640 | tf_op jit(solution)/shard_map/ppermute | solution.py:369
  47.5 0.0 copy-done.1
  47.5 4.9 %shard_map.67 = (f32[4,128,128]{2,1,0:T(8,128)S(1)}, f32[2,4,192,128]{3,2,1,0:T(8,128)S(1)}, f32[6,32,128]{2,1,0:T(8,128)S(1)}, f32[6,32,128]{2,1,0:T(8,128)S(1)}) custom-call(f32[2,4,192,128]{3,2,1,0:T(8,128)S(1)} %get-tuple-element.23.b_ref, f32[2,4,192,128]{3,2,1,0:T(8,128)S(1)} %get-tuple-element.27.sum_ref, ...), custom_call_target="tpu_custom_call" | custom-call | tf_op jit(solution)/shard_map/pallas_call | solution.py:415
  52.5 2.4 %collective-permute-start.8 = (f32[6,32,128]{2,1,0:T(8,128)S(1)}, f32[6,32,128]{2,1,0:T(8,128)S(1)}, u32[]{:S(2)}, u32[]{:S(2)}) collective-permute-start(f32[6,32,128]{2,1,0:T(8,128)S(1)} %get-tuple-element.32), channel_id=1, source_target_pairs={{0,16},{16,32},{32,48},{48,64},{64,80},{80,96},{96,112},{112,128},... | collective-permute-start | bytes 294920 | tf_op jit(solution)/shard_map/ppermute | solution.py:369
  54.9 0.0 collective-permute-start.9
  54.9 1.6 %collective-permute-done.8.from_up_ref = f32[6,32,128]{2,1,0:T(8,128)S(1)} collective-permute-done((f32[6,32,128]{2,1,0:T(8,128)S(1)}, f32[6,32,128]{2,1,0:T(8,128)S(1)}, u32[]{:S(2)}, u32[]{:S(2)}) %collective-permute-start.8) | collective-permute-done | bytes 98336 | tf_op jit(solution)/shard_map/ppermute | solution.py:369
  56.5 6.0 %collective-permute-done.9.from_down_ref = f32[6,32,128]{2,1,0:T(8,128)S(1)} collective-permute-done((f32[6,32,128]{2,1,0:T(8,128)S(1)}, f32[6,32,128]{2,1,0:T(8,128)S(1)}, u32[]{:S(2)}, u32[]{:S(2)}) %collective-permute-start.9) | collective-permute-done | bytes 98336 | tf_op jit(solution)/shard_map/ppermute | solution.py:369
  62.5 0.2 shard_map.68
  62.7 0.7 %collective-permute-start.10 = (f32[128,128]{1,0:T(8,128)S(1)}, f32[128,128]{1,0:T(8,128)S(1)}, u32[]{:S(2)}, u32[]{:S(2)}) collective-permute-start(f32[128,128]{1,0:T(8,128)S(1)} %get-tuple-element.35), channel_id=1, source_target_pairs={{0,1},{1,2},{2,3},{3,4},{4,5},{5,6},{6,7},{7,8},{8,9},{9,10},{10,1... | collective-permute-start | bytes 196616 | tf_op jit(solution)/shard_map/ppermute | solution.py:369
  63.5 0.8 %collective-permute-start.11 = (f32[128,128]{1,0:T(8,128)S(1)}, f32[128,128]{1,0:T(8,128)S(1)}, u32[]{:S(2)}, u32[]{:S(2)}) collective-permute-start(f32[128,128]{1,0:T(8,128)S(1)} %get-tuple-element.36), channel_id=1, source_target_pairs={{0,15},{1,0},{2,1},{3,2},{4,3},{5,4},{6,5},{7,6},{8,7},{9,8},{10,9... | collective-permute-start | bytes 196616 | tf_op jit(solution)/shard_map/ppermute | solution.py:369
  64.3 1.6 %collective-permute-done.10.from_left_ref = f32[128,128]{1,0:T(8,128)S(1)} collective-permute-done((f32[128,128]{1,0:T(8,128)S(1)}, f32[128,128]{1,0:T(8,128)S(1)}, u32[]{:S(2)}, u32[]{:S(2)}) %collective-permute-start.10) | collective-permute-done | bytes 65568 | tf_op jit(solution)/shard_map/ppermute | solution.py:369
  65.9 2.8 %collective-permute-done.11.from_right_ref = f32[128,128]{1,0:T(8,128)S(1)} collective-permute-done((f32[128,128]{1,0:T(8,128)S(1)}, f32[128,128]{1,0:T(8,128)S(1)}, u32[]{:S(2)}, u32[]{:S(2)}) %collective-permute-start.11) | collective-permute-done | bytes 65568 | tf_op jit(solution)/shard_map/ppermute | solution.py:369
  68.7 0.9 %shard_map.69 = f32[4,128,128]{2,1,0:T(8,128)} custom-call(f32[4,128,128]{2,1,0:T(8,128)S(1)} %get-tuple-element.34.core_ref, f32[128,128]{1,0:T(8,128)S(1)} %collective-permute-done.10.from_left_ref, f32[128,128]{1,0:T(8,128)S(1)} %collective-permute-done.11.from_right_ref), custom_call_target="tpu_custom_call" | custom-call | tf_op jit(solution)/shard_map/pallas_call | solution.py:430
Async XLA Ops:
  0.0 8.3 %copy-start.2 = (f32[2,2,128,128]{3,2,1,0:T(8,128)S(1)}, f32[2,2,128,128]{3,2,1,0:T(8,128)}, u32[]{:S(2)}) copy-start(f32[2,2,128,128]{3,2,1,0:T(8,128)} %param.6) | copy-start | bytes 786436
  0.0 17.1 %copy-start.3 = (f32[1,1,6,128,128]{4,3,2,1,0:T(8,128)S(1)}, f32[1,1,6,128,128]{4,3,2,1,0:T(8,128)}, u32[]{:S(2)}) copy-start(f32[1,1,6,128,128]{4,3,2,1,0:T(8,128)} %param.8) | copy-start | bytes 1179652
  1.0 7.4 %collective-permute-start.1 = (f32[4,32,128]{2,1,0:T(8,128)S(1)}, f32[4,32,128]{2,1,0:T(8,128)S(1)}, u32[]{:S(2)}, u32[]{:S(2)}) collective-permute-start(f32[4,32,128]{2,1,0:T(8,128)S(1)} %get-tuple-element.37), channel_id=1, source_target_pairs={{0,240},{16,0},{32,16},{48,32},{64,48},{80,64},{96,80},{112,96},{1... | collective-permute-start | bytes 196616 | tf_op jit(solution)/shard_map/ppermute | solution.py:369
  1.7 6.6 %collective-permute-start = (f32[4,32,128]{2,1,0:T(8,128)S(1)}, f32[4,32,128]{2,1,0:T(8,128)S(1)}, u32[]{:S(2)}, u32[]{:S(2)}) collective-permute-start(f32[4,32,128]{2,1,0:T(8,128)S(1)} %get-tuple-element.38), channel_id=1, source_target_pairs={{0,16},{16,32},{32,48},{48,64},{64,80},{80,96},{96,112},{112,128},... | collective-permute-start | bytes 196616 | tf_op jit(solution)/shard_map/ppermute | solution.py:369
  8.6 4.5 %collective-permute-start.2 = (f32[192,128]{1,0:T(8,128)S(1)}, f32[192,128]{1,0:T(8,128)S(1)}, u32[]{:S(2)}, u32[]{:S(2)}) collective-permute-start(f32[192,128]{1,0:T(8,128)S(1)} %get-tuple-element.21), channel_id=1, source_target_pairs={{0,1},{1,2},{2,3},{3,4},{4,5},{5,6},{6,7},{7,8},{8,9},{9,10},{10,1... | collective-permute-start | bytes 294920 | tf_op jit(solution)/shard_map/ppermute | solution.py:369
  11.5 5.6 %collective-permute-start.3 = (f32[192,128]{1,0:T(8,128)S(1)}, f32[192,128]{1,0:T(8,128)S(1)}, u32[]{:S(2)}, u32[]{:S(2)}) collective-permute-start(f32[192,128]{1,0:T(8,128)S(1)} %get-tuple-element.22), channel_id=1, source_target_pairs={{0,15},{1,0},{2,1},{3,2},{4,3},{5,4},{6,5},{7,6},{8,7},{9,8},{10,9... | collective-permute-start | bytes 294920 | tf_op jit(solution)/shard_map/ppermute | solution.py:369
  12.1 0.7 copy-start.5
  17.1 1.2 %copy-start = (bf16[4,2,256,256]{3,2,1,0:T(8,128)(2,1)S(1)}, bf16[4,2,256,256]{3,2,1,0:T(8,128)(2,1)}, u32[]{:S(2)}) copy-start(bf16[4,2,256,256]{3,2,1,0:T(8,128)(2,1)} %constant.2.clone.w_ref) | copy-start | bytes 3145732
  18.3 0.9 %copy-start.4 = (f32[2,128,128]{2,1,0:T(8,128)S(1)}, f32[2,128,128]{2,1,0:T(8,128)}, u32[]{:S(2)}) copy-start(f32[2,128,128]{2,1,0:T(8,128)} %probe_ref.3) | copy-start | bytes 393220
  24.1 23.4 %copy-start.1 = (bf16[4,2,256,256]{3,2,1,0:T(8,128)(2,1)S(1)}, bf16[4,2,256,256]{3,2,1,0:T(8,128)(2,1)}, u32[]{:S(2)}) copy-start(bf16[4,2,256,256]{3,2,1,0:T(8,128)(2,1)} %constant.2.clone.w_ref) | copy-start | bytes 3145732
  24.1 11.2 %collective-permute-start.4 = (f32[6,64,128]{2,1,0:T(8,128)S(1)}, f32[6,64,128]{2,1,0:T(8,128)S(1)}, u32[]{:S(2)}, u32[]{:S(2)}) collective-permute-start(f32[6,64,128]{2,1,0:T(8,128)S(1)} %get-tuple-element.25), channel_id=1, source_target_pairs={{0,16},{16,32},{32,48},{48,64},{64,80},{80,96},{96,112},{112,128},... | collective-permute-start | bytes 589832 | tf_op jit(solution)/shard_map/ppermute | solution.py:369
  30.4 8.7 %collective-permute-start.5 = (f32[6,64,128]{2,1,0:T(8,128)S(1)}, f32[6,64,128]{2,1,0:T(8,128)S(1)}, u32[]{:S(2)}, u32[]{:S(2)}) collective-permute-start(f32[6,64,128]{2,1,0:T(8,128)S(1)} %get-tuple-element.26), channel_id=1, source_target_pairs={{0,240},{16,0},{32,16},{48,32},{64,48},{80,64},{96,80},{112,96},{1... | collective-permute-start | bytes 589832 | tf_op jit(solution)/shard_map/ppermute | solution.py:369
  39.3 5.4 %collective-permute-start.6 = (f32[2,192,128]{2,1,0:T(8,128)S(1)}, f32[2,192,128]{2,1,0:T(8,128)S(1)}, u32[]{:S(2)}, u32[]{:S(2)}) collective-permute-start(f32[2,192,128]{2,1,0:T(8,128)S(1)} %get-tuple-element.28), channel_id=1, source_target_pairs={{0,1},{1,2},{2,3},{3,4},{4,5},{5,6},{6,7},{7,8},{8,9},{9,10},{10,1... | collective-permute-start | bytes 589832 | tf_op jit(solution)/shard_map/ppermute | solution.py:369
  40.9 6.6 %collective-permute-start.7 = (f32[2,192,128]{2,1,0:T(8,128)S(1)}, f32[2,192,128]{2,1,0:T(8,128)S(1)}, u32[]{:S(2)}, u32[]{:S(2)}) collective-permute-start(f32[2,192,128]{2,1,0:T(8,128)S(1)} %get-tuple-element.29), channel_id=1, source_target_pairs={{0,15},{1,0},{2,1},{3,2},{4,3},{5,4},{6,5},{7,6},{8,7},{9,8},{10,9... | collective-permute-start | bytes 589832 | tf_op jit(solution)/shard_map/ppermute | solution.py:369
  52.5 4.0 %collective-permute-start.8 = (f32[6,32,128]{2,1,0:T(8,128)S(1)}, f32[6,32,128]{2,1,0:T(8,128)S(1)}, u32[]{:S(2)}, u32[]{:S(2)}) collective-permute-start(f32[6,32,128]{2,1,0:T(8,128)S(1)} %get-tuple-element.32), channel_id=1, source_target_pairs={{0,16},{16,32},{32,48},{48,64},{64,80},{80,96},{96,112},{112,128},... | collective-permute-start | bytes 294920 | tf_op jit(solution)/shard_map/ppermute | solution.py:369
  54.9 7.7 %collective-permute-start.9 = (f32[6,32,128]{2,1,0:T(8,128)S(1)}, f32[6,32,128]{2,1,0:T(8,128)S(1)}, u32[]{:S(2)}, u32[]{:S(2)}) collective-permute-start(f32[6,32,128]{2,1,0:T(8,128)S(1)} %get-tuple-element.33), channel_id=1, source_target_pairs={{0,240},{16,0},{32,16},{48,32},{64,48},{80,64},{96,80},{112,96},{1... | collective-permute-start | bytes 294920 | tf_op jit(solution)/shard_map/ppermute | solution.py:369
  62.7 3.2 %collective-permute-start.10 = (f32[128,128]{1,0:T(8,128)S(1)}, f32[128,128]{1,0:T(8,128)S(1)}, u32[]{:S(2)}, u32[]{:S(2)}) collective-permute-start(f32[128,128]{1,0:T(8,128)S(1)} %get-tuple-element.35), channel_id=1, source_target_pairs={{0,1},{1,2},{2,3},{3,4},{4,5},{5,6},{6,7},{7,8},{8,9},{9,10},{10,1... | collective-permute-start | bytes 196616 | tf_op jit(solution)/shard_map/ppermute | solution.py:369
  63.5 5.2 %collective-permute-start.11 = (f32[128,128]{1,0:T(8,128)S(1)}, f32[128,128]{1,0:T(8,128)S(1)}, u32[]{:S(2)}, u32[]{:S(2)}) collective-permute-start(f32[128,128]{1,0:T(8,128)S(1)} %get-tuple-element.36), channel_id=1, source_target_pairs={{0,15},{1,0},{2,1},{3,2},{4,3},{5,4},{6,5},{7,6},{8,7},{9,8},{10,9... | collective-permute-start | bytes 196616 | tf_op jit(solution)/shard_map/ppermute | solution.py:369
where the time goes:
time: 70.8 us; the launch traced here: 69.6 us
  waiting for transfers between devices  32.5 us (46%)
  starting transfers between devices  21.1 us (30%)
  Pallas kernels  11.4 us (16%)
  local copies, waits for them, and re-layouts  3.86 us (5%)
  between operations  0.72 us (1%)
    ppermute x12, waiting for transfers between devices, shifted(): lax.ppermute(value, axis, [(i, (i + by) % count) for i in range(count)])  32.5 us
    ppermute x12, starting transfers between devices, shifted(): lax.ppermute(value, axis, [(i, (i + by) % count) for i in range(count)])  21.1 us
    pallas_call x1, Pallas kernels, local(): call(second_kernel, [(4, size, size), full, (6, 32, size), (6, 32, size)]...  4.95 us
    pallas_call x1, Pallas kernels, local(): call(first_kernel, [full, full, (6, 64, size), (6, 64, size)], [VMEM] * 5...  4.91 us
    unnamed x12, local copies, waits for them, and re-layouts  2.82 us
  transfers between devices with their start and end apart: 12, of which 11 were waited for; matrix products, arithmetic and copies ran while one was open for 0% of the time, Pallas kernels for 0%

commit v1 on v0

--- a/solution.py
+++ b/solution.py
@@ -85,7 +85,30 @@
     return row > 0, row < rows - 1, col > 0, col < cols - 1
 
 
-def halo_pack_kernel(core_ref, above_ref, below_ref, left_ref, right_ref):
+def stage_kernel(probe_hbm, w_hbm, probe_ref, w_ref, sems):
+    copies = [
+        pltpu.make_async_copy(probe_hbm, probe_ref, sems.at[0]),
+        pltpu.make_async_copy(w_hbm, w_ref, sems.at[1]),
+    ]
+    for copy in copies:
+        copy.start()
+    for copy in copies:
+        copy.wait()
+
+
+def amplitude_kernel(intensity_ref, after_ref, amplitude_ref):
+    del after_ref
+
+    def root(s, carry):
+        measured = intensity_ref[s]
+        amplitude_ref[s] = measured * lax.rsqrt(measured)
+        return carry
+
+    lax.fori_loop(0, amplitude_ref.shape[0], root, 0)
+
+
+def halo_pack_kernel(core_ref, above_ref, below_ref, staged_ref, left_ref, right_ref):
+    del staged_ref
     has_up, has_down, _, _ = edges()
     parts = (
         (0, 32, above_ref, 0, has_up),
@@ -100,10 +123,10 @@
         right_ref[pl.ds(start, length), :] = pack_quarter(planes, 96)
 
 
-def gradients(b_ref, probe_ref, intensity_ref, live, offsets_ref, w_ref, g_ref, scratch):
+def gradients(b_ref, probe_ref, amplitude_ref, live, offsets_ref, w_ref, g_ref, scratch):
     win_ref, prop_ref, xh_ref, xl_ref, zh_ref, zl_ref = scratch
-    slots = intensity_ref.shape[0]
-    size = intensity_ref.shape[1]
+    slots = amplitude_ref.shape[0]
+    size = amplitude_ref.shape[1]
     lane = lane_iota(size)
     rows_at, shifts, first_masks = [], [], []
     for s in range(slots):
@@ -194,10 +217,8 @@
         put_x(s, real * a_real - imag * a_imag, real * a_imag + imag * a_real)
 
     def after_far(s, real, imag):
-        measured = intensity_ref[s]
-        amplitude = measured * lax.rsqrt(measured)
-        ratio = amplitude * lax.rsqrt(real * real + imag * imag + 1.0)
-        scale = 1.0 - ratio
+        magnitude = real * real + imag * imag + 1.0
+        scale = 1.0 - amplitude_ref[s] * lax.rsqrt(magnitude)
         put_x(s, real * scale, imag * scale)
 
     def after_back(s, real, imag):
@@ -239,7 +260,7 @@
 
 def first_kernel(
     core_ref, above_ref, below_ref, from_left_ref, from_right_ref,
-    probe_ref, intensity_ref, counts_ref, offsets_ref, w_ref,
+    probe_ref, amplitude_ref, counts_ref, offsets_ref, w_ref,
     b_ref, g_ref, up_ref, down_ref, *scratch,
 ):
     has_up, has_down, has_left, has_right = edges()
@@ -255,7 +276,7 @@
             lane, unpack_quarter(from_right, p, 0), unpack_quarter(from_left, p, 96)
         )
     gradients(
-        b_ref, probe_ref, intensity_ref, counts_ref[0, 0], offsets_ref, w_ref, g_ref, scratch
+        b_ref, probe_ref, amplitude_ref, counts_ref[0, 0], offsets_ref, w_ref, g_ref, scratch
     )
     row_pack(g_ref, 0, 64, up_ref)
     row_pack(g_ref, 128, 64, down_ref)
@@ -284,7 +305,7 @@
 
 def second_kernel(
     b_ref, sum_ref, from_left_ref, from_right_ref,
-    probe_ref, intensity_ref, counts_ref, offsets_ref, w_ref,
+    probe_ref, amplitude_ref, counts_ref, offsets_ref, w_ref,
     core_ref, g_ref, up_ref, down_ref, new_ref, *scratch,
 ):
     has_up, has_down, has_left, has_right = edges()
@@ -310,7 +331,7 @@
         new_ref[1, p] = jnp.where(inside_far, far, 0.0)
         core_ref[p] = near[32:160]
     gradients(
-        new_ref, probe_ref, intensity_ref, counts_ref[0, 0], offsets_ref, w_ref, g_ref, scratch
+        new_ref, probe_ref, amplitude_ref, counts_ref[0, 0], offsets_ref, w_ref, g_ref, scratch
     )
     row_pack(g_ref, 0, 32, up_ref)
     row_pack(g_ref, 160, 32, down_ref)
@@ -352,15 +373,23 @@
 SMEM = pl.BlockSpec(memory_space=pltpu.SMEM)
 
 
-def call(kernel, outs, specs, limit, scratch=()):
-    shapes = [jax.ShapeDtypeStruct(shape, jnp.float32) for shape in outs]
+ANY = pl.BlockSpec(memory_space=pl.ANY)
+HBM = pl.BlockSpec(memory_space=pltpu.HBM)
+
+
+def call(kernel, outs, specs, limit, scratch=(), cost=None):
+    shapes = [
+        out if isinstance(out, jax.ShapeDtypeStruct) else jax.ShapeDtypeStruct(out, jnp.float32)
+        for out in outs
+    ]
     return pl.pallas_call(
         kernel,
         out_shape=shapes,
         in_specs=specs,
         out_specs=[VMEM] * len(outs),
         scratch_shapes=list(scratch),
-        compiler_params=pltpu.CompilerParams(vmem_limit_bytes=limit << 20),
+        compiler_params=pltpu.CompilerParams(vmem_limit_bytes=int(limit * 2**20)),
+        cost_estimate=cost,
     )
 
 
@@ -383,7 +412,6 @@
     core = object_field.reshape(4, size, size)
     own_intensity = intensity[0, 0]
     own_offsets = offsets[0, 0]
-    common = (probe_field, own_intensity, counts, own_offsets, weights)
     common_specs = [VMEM, VMEM, SMEM, SMEM, VMEM]
     scratch = (
         pltpu.VMEM((4, slots, size, size), jnp.float32),
@@ -396,15 +424,31 @@
     full = (2, 4, tall, size)
 
     above, below = exchange("row", core[:, :BORDER], core[:, size - BORDER :])
+    probe, weights = call(
+        stage_kernel,
+        [probe_field.shape, jax.ShapeDtypeStruct(weights.shape, weights.dtype)],
+        [HBM] * 2,
+        8,
+        (pltpu.SemaphoreType.DMA((2,)),),
+        pl.CostEstimate(flops=0, bytes_accessed=2400000, transcendentals=0),
+    )(probe_field, weights)
     to_left, to_right = call(
-        halo_pack_kernel, [(tall, LANES)] * 2, [VMEM] * 3, 8
-    )(core, above, below)
+        halo_pack_kernel, [(tall, LANES)] * 2, [VMEM] * 3 + [ANY], 8
+    )(core, above, below, probe)
     left, right = exchange("col", to_left, to_right)
+    (amplitude,) = call(
+        amplitude_kernel,
+        [own_intensity.shape],
+        [VMEM, ANY],
+        8,
+        cost=pl.CostEstimate(flops=200000, bytes_accessed=800000, transcendentals=100000),
+    )(own_intensity, to_left)
+    common = (probe, amplitude, counts, own_offsets, weights)
     bordered, grads, up, down = call(
         first_kernel,
         [full, full, (6, 64, size), (6, 64, size)],
         [VMEM] * 5 + common_specs,
-        32,
+        20,
         scratch,
     )(core, above, below, left, right, *common)
     from_up, from_down = exchange("row", up, down)
@@ -416,7 +460,7 @@
         second_kernel,
         [(4, size, size), full, (6, 32, size), (6, 32, size)],
         [VMEM] * 4 + common_specs,
-        32,
+        20,
         (pltpu.VMEM(full, jnp.float32),) + scratch,
     )(bordered, summed, left, right, *common)
     from_up, from_down = exchange("row", up, down)

time: 70.8 us -> 68.4 us (0.966)
  waiting for transfers between devices: 32.5 us -> 31.1 us
  local copies, waits for them, and re-layouts: 3.86 us -> 2.92 us
    ppermute x12, waiting for transfers between devices: 32.5 us -> 31.1 us  [shifted(): lax.ppermute(value, axis, [(i, (i + by) % count) for i in range(count)])]
    unnamed x12 -> x10, local copies, waits for them, and re-layouts: 2.82 us -> 1.91 us
where the time goes in v1:
time: 68.4 us; the launch traced here: 67.2 us
  waiting for transfers between devices  31.1 us (45%)
  starting transfers between devices  21.1 us (31%)
  Pallas kernels  11.5 us (17%)
  local copies, waits for them, and re-layouts  2.92 us (4%)
  between operations  0.74 us (1%)
    ppermute x12, waiting for transfers between devices, shifted(): lax.ppermute(value, axis, [(i, (i + by) % count) for i in range(count)])  31.1 us
    ppermute x12, starting transfers between devices, shifted(): lax.ppermute(value, axis, [(i, (i + by) % count) for i in range(count)])  21.1 us
    pallas_call x1, Pallas kernels, local(): call(second_kernel, [(4, size, size), full, (6, 32, size), (6, 32, size)]...  4.85 us
    pallas_call x1, Pallas kernels, local(): call(first_kernel, [full, full, (6, 64, size), (6, 64, size)], [VMEM] * 5...  4.76 us
    unnamed x10, local copies, waits for them, and re-layouts  1.91 us
  transfers between devices with their start and end apart: 12, of which 11 were waited for; matrix products, arithmetic and copies ran while one was open for 0% of the time, Pallas kernels for 0%

profile of v1, /device:TPU:123, one launch (start us, length us, event | category | flops | bytes accessed | tf_op | source)
XLA Modules:
  0.0 67.2 jit_solution(12728884352788368356)
XLA Ops:
  0.0 0.0 copy-start.3
  0.0 0.9 %fusion = (f32[4,32,128]{2,1,0:T(8,128)S(1)}, f32[4,32,128]{2,1,0:T(8,128)S(1)}) fusion(f32[4,128,128]{2,1,0:T(8,128)} %bitcast.4), kind=kLoop, calls=%fused_computation | loop fusion | bytes 262144 | tf_op jit(solution)/shard_map/slice | solution.py:426
  0.9 0.8 %collective-permute-start.1 = (f32[4,32,128]{2,1,0:T(8,128)S(1)}, f32[4,32,128]{2,1,0:T(8,128)S(1)}, u32[]{:S(2)}, u32[]{:S(2)}) collective-permute-start(f32[4,32,128]{2,1,0:T(8,128)S(1)} %get-tuple-element.41), channel_id=1, source_target_pairs={{0,240},{16,0},{32,16},{48,32},{64,48},{80,64},{96,80},{112,96},{1... | collective-permute-start | bytes 196616 | tf_op jit(solution)/shard_map/ppermute | solution.py:398
  1.7 0.0 copy-start
  1.7 4.7 %collective-permute-start = (f32[4,32,128]{2,1,0:T(8,128)S(1)}, f32[4,32,128]{2,1,0:T(8,128)S(1)}, u32[]{:S(2)}, u32[]{:S(2)}) collective-permute-start(f32[4,32,128]{2,1,0:T(8,128)S(1)} %get-tuple-element.42), channel_id=1, source_target_pairs={{0,16},{16,32},{32,48},{48,64},{64,80},{80,96},{96,112},{112,128},... | collective-permute-start | bytes 196616 | tf_op jit(solution)/shard_map/ppermute | solution.py:398
  6.4 0.0 copy-done.3
  6.4 0.0 copy-start.1
  6.4 1.2 %copy-done.1 = bf16[4,2,256,256]{3,2,1,0:T(8,128)(2,1)S(1)} copy-done((bf16[4,2,256,256]{3,2,1,0:T(8,128)(2,1)S(1)}, bf16[4,2,256,256]{3,2,1,0:T(8,128)(2,1)}, u32[]{:S(2)}) %copy-start.1) | copy-done | bytes 1048600
  7.6 0.2 shard_map.64
  7.8 0.0 copy-start.2
  7.8 0.5 collective-permute-done.1.below_ref
  8.3 0.0 collective-permute-done.above_ref
  8.3 0.0 copy-done
  8.3 0.2 shard_map.65
  8.5 2.9 %collective-permute-start.2 = (f32[192,128]{1,0:T(8,128)S(1)}, f32[192,128]{1,0:T(8,128)S(1)}, u32[]{:S(2)}, u32[]{:S(2)}) collective-permute-start(f32[192,128]{1,0:T(8,128)S(1)} %get-tuple-element.24), channel_id=1, source_target_pairs={{0,1},{1,2},{2,3},{3,4},{4,5},{5,6},{6,7},{7,8},{8,9},{9,10},{10,1... | collective-permute-start | bytes 294920 | tf_op jit(solution)/shard_map/ppermute | solution.py:398
  11.4 0.0 collective-permute-start.3
  12.1 0.0 copy-start.4
  12.1 0.7 copy-done.4
  12.8 0.1 copy.7.offsets_ref
  12.9 0.0 copy-done.2
  12.9 0.1 shard_map.66.amplitude_ref
  13.0 0.1 collective-permute-done.2.from_left_ref
  13.1 3.9 %collective-permute-done.3.from_right_ref = f32[192,128]{1,0:T(8,128)S(1)} collective-permute-done((f32[192,128]{1,0:T(8,128)S(1)}, f32[192,128]{1,0:T(8,128)S(1)}, u32[]{:S(2)}, u32[]{:S(2)}) %collective-permute-start.3) | collective-permute-done | bytes 98336 | tf_op jit(solution)/shard_map/ppermute | solution.py:398
  17.0 4.8 %shard_map.67 = (f32[2,4,192,128]{3,2,1,0:T(8,128)S(1)}, f32[2,4,192,128]{3,2,1,0:T(8,128)S(1)}, f32[6,64,128]{2,1,0:T(8,128)S(1)}, f32[6,64,128]{2,1,0:T(8,128)S(1)}) custom-call(f32[4,128,128]{2,1,0:T(8,128)S(1)} %bitcast.6, f32[4,32,128]{2,1,0:T(8,128)S(1)} %collective-permute-done.above_ref, f32[4,32,128]{2,1,0:T(8,128)S(1)} %collective-permute-done.1.below_ref, ...), custom_call_target="tpu_custom_call" | custom-call | tf_op jit(solution)/shard_map/pallas_call | solution.py:447
  21.8 6.3 %collective-permute-start.4 = (f32[6,64,128]{2,1,0:T(8,128)S(1)}, f32[6,64,128]{2,1,0:T(8,128)S(1)}, u32[]{:S(2)}, u32[]{:S(2)}) collective-permute-start(f32[6,64,128]{2,1,0:T(8,128)S(1)} %get-tuple-element.29), channel_id=1, source_target_pairs={{0,16},{16,32},{32,48},{48,64},{64,80},{80,96},{96,112},{112,128},... | collective-permute-start | bytes 589832 | tf_op jit(solution)/shard_map/ppermute | solution.py:398
  28.1 0.0 collective-permute-start.5
  28.1 5.0 %collective-permute-done.4.from_up_ref = f32[6,64,128]{2,1,0:T(8,128)S(1)} collective-permute-done((f32[6,64,128]{2,1,0:T(8,128)S(1)}, f32[6,64,128]{2,1,0:T(8,128)S(1)}, u32[]{:S(2)}, u32[]{:S(2)}) %collective-permute-start.4) | collective-permute-done | bytes 196640 | tf_op jit(solution)/shard_map/ppermute | solution.py:398
  33.0 3.7 %collective-permute-done.5.from_down_ref = f32[6,64,128]{2,1,0:T(8,128)S(1)} collective-permute-done((f32[6,64,128]{2,1,0:T(8,128)S(1)}, f32[6,64,128]{2,1,0:T(8,128)S(1)}, u32[]{:S(2)}, u32[]{:S(2)}) %collective-permute-start.5) | collective-permute-done | bytes 196640 | tf_op jit(solution)/shard_map/ppermute | solution.py:398
  36.8 0.2 shard_map.68
  37.0 1.6 %collective-permute-start.6 = (f32[2,192,128]{2,1,0:T(8,128)S(1)}, f32[2,192,128]{2,1,0:T(8,128)S(1)}, u32[]{:S(2)}, u32[]{:S(2)}) collective-permute-start(f32[2,192,128]{2,1,0:T(8,128)S(1)} %get-tuple-element.32), channel_id=1, source_target_pairs={{0,1},{1,2},{2,3},{3,4},{4,5},{5,6},{6,7},{7,8},{8,9},{9,10},{10,1... | collective-permute-start | bytes 589832 | tf_op jit(solution)/shard_map/ppermute | solution.py:398
  38.6 1.0 %collective-permute-start.7 = (f32[2,192,128]{2,1,0:T(8,128)S(1)}, f32[2,192,128]{2,1,0:T(8,128)S(1)}, u32[]{:S(2)}, u32[]{:S(2)}) collective-permute-start(f32[2,192,128]{2,1,0:T(8,128)S(1)} %get-tuple-element.33), channel_id=1, source_target_pairs={{0,15},{1,0},{2,1},{3,2},{4,3},{5,4},{6,5},{7,6},{8,7},{9,8},{10,9... | collective-permute-start | bytes 589832 | tf_op jit(solution)/shard_map/ppermute | solution.py:398
  39.6 2.8 %collective-permute-done.6.from_left_ref = f32[2,192,128]{2,1,0:T(8,128)S(1)} collective-permute-done((f32[2,192,128]{2,1,0:T(8,128)S(1)}, f32[2,192,128]{2,1,0:T(8,128)S(1)}, u32[]{:S(2)}, u32[]{:S(2)}) %collective-permute-start.6) | collective-permute-done | bytes 196640 | tf_op jit(solution)/shard_map/ppermute | solution.py:398
  42.4 2.9 %collective-permute-done.7.from_right_ref = f32[2,192,128]{2,1,0:T(8,128)S(1)} collective-permute-done((f32[2,192,128]{2,1,0:T(8,128)S(1)}, f32[2,192,128]{2,1,0:T(8,128)S(1)}, u32[]{:S(2)}, u32[]{:S(2)}) %collective-permute-start.7) | collective-permute-done | bytes 196640 | tf_op jit(solution)/shard_map/ppermute | solution.py:398
  45.3 4.8 %shard_map.69 = (f32[4,128,128]{2,1,0:T(8,128)S(1)}, f32[2,4,192,128]{3,2,1,0:T(8,128)S(1)}, f32[6,32,128]{2,1,0:T(8,128)S(1)}, f32[6,32,128]{2,1,0:T(8,128)S(1)}) custom-call(f32[2,4,192,128]{3,2,1,0:T(8,128)S(1)} %get-tuple-element.27.b_ref, f32[2,4,192,128]{3,2,1,0:T(8,128)S(1)} %get-tuple-element.31.sum_ref, ...), custom_call_target="tpu_custom_call" | custom-call | tf_op jit(solution)/shard_map/pallas_call | solution.py:459
  50.1 2.3 %collective-permute-start.8 = (f32[6,32,128]{2,1,0:T(8,128)S(1)}, f32[6,32,128]{2,1,0:T(8,128)S(1)}, u32[]{:S(2)}, u32[]{:S(2)}) collective-permute-start(f32[6,32,128]{2,1,0:T(8,128)S(1)} %get-tuple-element.36), channel_id=1, source_target_pairs={{0,16},{16,32},{32,48},{48,64},{64,80},{80,96},{96,112},{112,128},... | collective-permute-start | bytes 294920 | tf_op jit(solution)/shard_map/ppermute | solution.py:398
  52.4 0.0 collective-permute-start.9
  52.4 1.6 %collective-permute-done.8.from_up_ref = f32[6,32,128]{2,1,0:T(8,128)S(1)} collective-permute-done((f32[6,32,128]{2,1,0:T(8,128)S(1)}, f32[6,32,128]{2,1,0:T(8,128)S(1)}, u32[]{:S(2)}, u32[]{:S(2)}) %collective-permute-start.8) | collective-permute-done | bytes 98336 | tf_op jit(solution)/shard_map/ppermute | solution.py:398
  54.1 6.0 %collective-permute-done.9.from_down_ref = f32[6,32,128]{2,1,0:T(8,128)S(1)} collective-permute-done((f32[6,32,128]{2,1,0:T(8,128)S(1)}, f32[6,32,128]{2,1,0:T(8,128)S(1)}, u32[]{:S(2)}, u32[]{:S(2)}) %collective-permute-start.9) | collective-permute-done | bytes 98336 | tf_op jit(solution)/shard_map/ppermute | solution.py:398
  60.1 0.2 shard_map.70
  60.3 0.8 %collective-permute-start.10 = (f32[128,128]{1,0:T(8,128)S(1)}, f32[128,128]{1,0:T(8,128)S(1)}, u32[]{:S(2)}, u32[]{:S(2)}) collective-permute-start(f32[128,128]{1,0:T(8,128)S(1)} %get-tuple-element.39), channel_id=1, source_target_pairs={{0,1},{1,2},{2,3},{3,4},{4,5},{5,6},{6,7},{7,8},{8,9},{9,10},{10,1... | collective-permute-start | bytes 196616 | tf_op jit(solution)/shard_map/ppermute | solution.py:398
  61.1 0.7 %collective-permute-start.11 = (f32[128,128]{1,0:T(8,128)S(1)}, f32[128,128]{1,0:T(8,128)S(1)}, u32[]{:S(2)}, u32[]{:S(2)}) collective-permute-start(f32[128,128]{1,0:T(8,128)S(1)} %get-tuple-element.40), channel_id=1, source_target_pairs={{0,15},{1,0},{2,1},{3,2},{4,3},{5,4},{6,5},{7,6},{8,7},{9,8},{10,9... | collective-permute-start | bytes 196616 | tf_op jit(solution)/shard_map/ppermute | solution.py:398
  61.8 1.6 %collective-permute-done.10.from_left_ref = f32[128,128]{1,0:T(8,128)S(1)} collective-permute-done((f32[128,128]{1,0:T(8,128)S(1)}, f32[128,128]{1,0:T(8,128)S(1)}, u32[]{:S(2)}, u32[]{:S(2)}) %collective-permute-start.10) | collective-permute-done | bytes 65568 | tf_op jit(solution)/shard_map/ppermute | solution.py:398
  63.5 2.9 %collective-permute-done.11.from_right_ref = f32[128,128]{1,0:T(8,128)S(1)} collective-permute-done((f32[128,128]{1,0:T(8,128)S(1)}, f32[128,128]{1,0:T(8,128)S(1)}, u32[]{:S(2)}, u32[]{:S(2)}) %collective-permute-start.11) | collective-permute-done | bytes 65568 | tf_op jit(solution)/shard_map/ppermute | solution.py:398
  66.4 0.9 %shard_map.71 = f32[4,128,128]{2,1,0:T(8,128)} custom-call(f32[4,128,128]{2,1,0:T(8,128)S(1)} %get-tuple-element.38.core_ref, f32[128,128]{1,0:T(8,128)S(1)} %collective-permute-done.10.from_left_ref, f32[128,128]{1,0:T(8,128)S(1)} %collective-permute-done.11.from_right_ref), custom_call_target="tpu_custom_call" | custom-call | tf_op jit(solution)/shard_map/pallas_call | solution.py:474
Async XLA Ops:
  0.0 6.4 %copy-start.3 = (f32[2,128,128]{2,1,0:T(8,128)S(1)}, f32[2,128,128]{2,1,0:T(8,128)}, u32[]{:S(2)}) copy-start(f32[2,128,128]{2,1,0:T(8,128)} %probe_hbm.1) | copy-start | bytes 393220
  0.9 7.4 %collective-permute-start.1 = (f32[4,32,128]{2,1,0:T(8,128)S(1)}, f32[4,32,128]{2,1,0:T(8,128)S(1)}, u32[]{:S(2)}, u32[]{:S(2)}) collective-permute-start(f32[4,32,128]{2,1,0:T(8,128)S(1)} %get-tuple-element.41), channel_id=1, source_target_pairs={{0,240},{16,0},{32,16},{48,32},{64,48},{80,64},{96,80},{112,96},{1... | collective-permute-start | bytes 196616 | tf_op jit(solution)/shard_map/ppermute | solution.py:398
  1.7 6.6 %copy-start = (f32[2,2,128,128]{3,2,1,0:T(8,128)S(1)}, f32[2,2,128,128]{3,2,1,0:T(8,128)}, u32[]{:S(2)}) copy-start(f32[2,2,128,128]{3,2,1,0:T(8,128)} %param.6) | copy-start | bytes 786436
  1.7 6.6 %collective-permute-start = (f32[4,32,128]{2,1,0:T(8,128)S(1)}, f32[4,32,128]{2,1,0:T(8,128)S(1)}, u32[]{:S(2)}, u32[]{:S(2)}) collective-permute-start(f32[4,32,128]{2,1,0:T(8,128)S(1)} %get-tuple-element.42), channel_id=1, source_target_pairs={{0,16},{16,32},{32,48},{48,64},{64,80},{80,96},{96,112},{112,128},... | collective-permute-start | bytes 196616 | tf_op jit(solution)/shard_map/ppermute | solution.py:398
  6.4 1.2 %copy-start.1 = (bf16[4,2,256,256]{3,2,1,0:T(8,128)(2,1)S(1)}, bf16[4,2,256,256]{3,2,1,0:T(8,128)(2,1)}, u32[]{:S(2)}) copy-start(bf16[4,2,256,256]{3,2,1,0:T(8,128)(2,1)} %constant.2.clone.w_hbm) | copy-start | bytes 3145732
  7.8 5.1 %copy-start.2 = (f32[1,1,6,128,128]{4,3,2,1,0:T(8,128)S(1)}, f32[1,1,6,128,128]{4,3,2,1,0:T(8,128)}, u32[]{:S(2)}) copy-start(f32[1,1,6,128,128]{4,3,2,1,0:T(8,128)} %param.8) | copy-start | bytes 1179652
  8.5 4.5 %collective-permute-start.2 = (f32[192,128]{1,0:T(8,128)S(1)}, f32[192,128]{1,0:T(8,128)S(1)}, u32[]{:S(2)}, u32[]{:S(2)}) collective-permute-start(f32[192,128]{1,0:T(8,128)S(1)} %get-tuple-element.24), channel_id=1, source_target_pairs={{0,1},{1,2},{2,3},{3,4},{4,5},{5,6},{6,7},{7,8},{8,9},{9,10},{10,1... | collective-permute-start | bytes 294920 | tf_op jit(solution)/shard_map/ppermute | solution.py:398
  11.4 5.6 %collective-permute-start.3 = (f32[192,128]{1,0:T(8,128)S(1)}, f32[192,128]{1,0:T(8,128)S(1)}, u32[]{:S(2)}, u32[]{:S(2)}) collective-permute-start(f32[192,128]{1,0:T(8,128)S(1)} %get-tuple-element.25.after_ref), channel_id=1, source_target_pairs={{0,15},{1,0},{2,1},{3,2},{4,3},{5,4},{6,5},{7,6},{8,7},{9,8},{10,9... | collective-permute-start | bytes 294920 | tf_op jit(solution)/shard_map/ppermute | solution.py:398
  12.1 0.7 %copy-start.4 = (s32[1,1,6,2]{2,3,1,0:T(2,128)S(1)}, s32[1,1,6,2]{2,3,1,0:T(2,128)}, u32[]{:S(2)}) copy-start(s32[1,1,6,2]{2,3,1,0:T(2,128)} %param.10) | copy-start | bytes 148
  21.8 11.2 %collective-permute-start.4 = (f32[6,64,128]{2,1,0:T(8,128)S(1)}, f32[6,64,128]{2,1,0:T(8,128)S(1)}, u32[]{:S(2)}, u32[]{:S(2)}) collective-permute-start(f32[6,64,128]{2,1,0:T(8,128)S(1)} %get-tuple-element.29), channel_id=1, source_target_pairs={{0,16},{16,32},{32,48},{48,64},{64,80},{80,96},{96,112},{112,128},... | collective-permute-start | bytes 589832 | tf_op jit(solution)/shard_map/ppermute | solution.py:398
  28.1 8.7 %collective-permute-start.5 = (f32[6,64,128]{2,1,0:T(8,128)S(1)}, f32[6,64,128]{2,1,0:T(8,128)S(1)}, u32[]{:S(2)}, u32[]{:S(2)}) collective-permute-start(f32[6,64,128]{2,1,0:T(8,128)S(1)} %get-tuple-element.30), channel_id=1, source_target_pairs={{0,240},{16,0},{32,16},{48,32},{64,48},{80,64},{96,80},{112,96},{1... | collective-permute-start | bytes 589832 | tf_op jit(solution)/shard_map/ppermute | solution.py:398
  37.0 5.4 %collective-permute-start.6 = (f32[2,192,128]{2,1,0:T(8,128)S(1)}, f32[2,192,128]{2,1,0:T(8,128)S(1)}, u32[]{:S(2)}, u32[]{:S(2)}) collective-permute-start(f32[2,192,128]{2,1,0:T(8,128)S(1)} %get-tuple-element.32), channel_id=1, source_target_pairs={{0,1},{1,2},{2,3},{3,4},{4,5},{5,6},{6,7},{7,8},{8,9},{9,10},{10,1... | collective-permute-start | bytes 589832 | tf_op jit(solution)/shard_map/ppermute | solution.py:398
  38.6 6.6 %collective-permute-start.7 = (f32[2,192,128]{2,1,0:T(8,128)S(1)}, f32[2,192,128]{2,1,0:T(8,128)S(1)}, u32[]{:S(2)}, u32[]{:S(2)}) collective-permute-start(f32[2,192,128]{2,1,0:T(8,128)S(1)} %get-tuple-element.33), channel_id=1, source_target_pairs={{0,15},{1,0},{2,1},{3,2},{4,3},{5,4},{6,5},{7,6},{8,7},{9,8},{10,9... | collective-permute-start | bytes 589832 | tf_op jit(solution)/shard_map/ppermute | solution.py:398
  50.1 4.0 %collective-permute-start.8 = (f32[6,32,128]{2,1,0:T(8,128)S(1)}, f32[6,32,128]{2,1,0:T(8,128)S(1)}, u32[]{:S(2)}, u32[]{:S(2)}) collective-permute-start(f32[6,32,128]{2,1,0:T(8,128)S(1)} %get-tuple-element.36), channel_id=1, source_target_pairs={{0,16},{16,32},{32,48},{48,64},{64,80},{80,96},{96,112},{112,128},... | collective-permute-start | bytes 294920 | tf_op jit(solution)/shard_map/ppermute | solution.py:398
  52.4 7.7 %collective-permute-start.9 = (f32[6,32,128]{2,1,0:T(8,128)S(1)}, f32[6,32,128]{2,1,0:T(8,128)S(1)}, u32[]{:S(2)}, u32[]{:S(2)}) collective-permute-start(f32[6,32,128]{2,1,0:T(8,128)S(1)} %get-tuple-element.37), channel_id=1, source_target_pairs={{0,240},{16,0},{32,16},{48,32},{64,48},{80,64},{96,80},{112,96},{1... | collective-permute-start | bytes 294920 | tf_op jit(solution)/shard_map/ppermute | solution.py:398
  60.3 3.2 %collective-permute-start.10 = (f32[128,128]{1,0:T(8,128)S(1)}, f32[128,128]{1,0:T(8,128)S(1)}, u32[]{:S(2)}, u32[]{:S(2)}) collective-permute-start(f32[128,128]{1,0:T(8,128)S(1)} %get-tuple-element.39), channel_id=1, source_target_pairs={{0,1},{1,2},{2,3},{3,4},{4,5},{5,6},{6,7},{7,8},{8,9},{9,10},{10,1... | collective-permute-start | bytes 196616 | tf_op jit(solution)/shard_map/ppermute | solution.py:398
  61.1 5.2 %collective-permute-start.11 = (f32[128,128]{1,0:T(8,128)S(1)}, f32[128,128]{1,0:T(8,128)S(1)}, u32[]{:S(2)}, u32[]{:S(2)}) collective-permute-start(f32[128,128]{1,0:T(8,128)S(1)} %get-tuple-element.40), channel_id=1, source_target_pairs={{0,15},{1,0},{2,1},{3,2},{4,3},{5,4},{6,5},{7,6},{8,7},{9,8},{10,9... | collective-permute-start | bytes 196616 | tf_op jit(solution)/shard_map/ppermute | solution.py:398

commit v2 on v1

--- a/solution.py
+++ b/solution.py
@@ -83,6 +83,20 @@
     rows = lax.axis_size("row")
     cols = lax.axis_size("col")
     return row > 0, row < rows - 1, col > 0, col < cols - 1
+
+
+def strips_kernel(core_hbm, top_ref, bottom_ref, sems):
+    size = core_hbm.shape[1]
+    copies = [
+        pltpu.make_async_copy(core_hbm.at[:, pl.ds(0, BORDER)], top_ref, sems.at[0]),
+        pltpu.make_async_copy(
+            core_hbm.at[:, pl.ds(size - BORDER, BORDER)], bottom_ref, sems.at[1]
+        ),
+    ]
+    for copy in copies:
+        copy.start()
+    for copy in copies:
+        copy.wait()
 
 
 def stage_kernel(probe_hbm, w_hbm, probe_ref, w_ref, sems):
@@ -359,14 +373,19 @@
         left_ref[pl.ds(start, length), :] = pack_quarter(far, 96)
 
 
-def final_kernel(core_ref, from_left_ref, from_right_ref, out_ref):
+def final_kernel(core_ref, from_left_ref, from_right_ref, out_hbm, done_ref, sems):
     _, _, has_left, has_right = edges()
     lane = lane_iota(core_ref.shape[1])
     left = jnp.where(has_left, from_left_ref[...], 0.0)
     right = jnp.where(has_right, from_right_ref[...], 0.0)
+    copies = []
     for p in range(4):
         added = outer(lane, unpack_quarter(left, p, 0), unpack_quarter(right, p, 96))
-        out_ref[p] = core_ref[p] - step_size * added
+        done_ref[p] = core_ref[p] - step_size * added
+        copies.append(pltpu.make_async_copy(done_ref.at[p], out_hbm.at[p], sems.at[p]))
+        copies[p].start()
+    for copy in copies:
+        copy.wait()
 
 
 VMEM = pl.BlockSpec(memory_space=pltpu.VMEM)
@@ -377,7 +396,7 @@
 HBM = pl.BlockSpec(memory_space=pltpu.HBM)
 
 
-def call(kernel, outs, specs, limit, scratch=(), cost=None):
+def call(kernel, outs, specs, limit, scratch=(), cost=None, out_spec=None):
     shapes = [
         out if isinstance(out, jax.ShapeDtypeStruct) else jax.ShapeDtypeStruct(out, jnp.float32)
         for out in outs
@@ -386,7 +405,7 @@
         kernel,
         out_shape=shapes,
         in_specs=specs,
-        out_specs=[VMEM] * len(outs),
+        out_specs=[out_spec or VMEM] * len(outs),
         scratch_shapes=list(scratch),
         compiler_params=pltpu.CompilerParams(vmem_limit_bytes=int(limit * 2**20)),
         cost_estimate=cost,
@@ -423,7 +442,14 @@
     )
     full = (2, 4, tall, size)
 
-    above, below = exchange("row", core[:, :BORDER], core[:, size - BORDER :])
+    top, bottom = call(
+        strips_kernel,
+        [(4, BORDER, size)] * 2,
+        [HBM],
+        4,
+        (pltpu.SemaphoreType.DMA((2,)),),
+    )(pltpu.with_memory_space_constraint(core, pltpu.HBM))
+    above, below = exchange("row", top, bottom)
     probe, weights = call(
         stage_kernel,
         [probe_field.shape, jax.ShapeDtypeStruct(weights.shape, weights.dtype)],
@@ -471,7 +497,14 @@
         16,
     )(core, grads, from_up, from_down)
     left, right = exchange("col", to_left, to_right)
-    (result,) = call(final_kernel, [(4, size, size)], [VMEM] * 3, 8)(core, left, right)
+    (result,) = call(
+        final_kernel,
+        [(4, size, size)],
+        [VMEM] * 3,
+        8,
+        (pltpu.VMEM((4, size, size), jnp.float32), pltpu.SemaphoreType.DMA((4,))),
+        out_spec=HBM,
+    )(core, left, right)
     return result.reshape(2, 2, size, size)
 
 

time: 68.4 us -> 67.1 us (0.981); the launches traced: 67.2 us -> 66.9 us
  starting transfers between devices: 21.1 us -> 12 us
  waiting for transfers between devices: 31.1 us -> 39.7 us
  local copies, waits for them, and re-layouts: 2.92 us -> 2.04 us
  Pallas kernels: 11.5 us -> 12.3 us
    ppermute x12, starting transfers between devices: 21.1 us -> 12 us  [shifted(): lax.ppermute(value, axis, [(i, (i + by) % count) for i in range(count)])]
    ppermute x12, waiting for transfers between devices: 31.1 us -> 39.7 us  [shifted(): lax.ppermute(value, axis, [(i, (i + by) % count) for i in range(count)])]
    slice x1 -> x0, local copies, waits for them, and re-layouts: 0.92 us -> none  [local(): above, below = exchange('row', core[:, :BORDER], core[:, size - BORDER:])]
    pallas_call x1 -> x2, Pallas kernels: 0.87 us -> 1.76 us  [the longest x1 0.92 us: local(): call(strips_kernel, [(4, BORDER, size)] * 2, [HBM], 4, (pltpu.SemaphoreTy...]
where the time goes in v2:
time: 67.1 us; the launch traced here: 66.9 us
  waiting for transfers between devices  39.7 us (59%)
  Pallas kernels  12.3 us (18%)
  starting transfers between devices  12 us (18%)
  local copies, waits for them, and re-layouts  2.04 us (3%)
  between operations  0.92 us (1%)
    ppermute x12, waiting for transfers between devices, shifted(): lax.ppermute(value, axis, [(i, (i + by) % count) for i in range(count)])  39.7 us
    ppermute x12, starting transfers between devices, shifted(): lax.ppermute(value, axis, [(i, (i + by) % count) for i in range(count)])  12 us
    pallas_call x1, Pallas kernels, local(): call(second_kernel, [(4, size, size), full, (6, 32, size), (6, 32, size)]...  4.81 us
    pallas_call x1, Pallas kernels, local(): call(first_kernel, [full, full, (6, 64, size), (6, 64, size)], [VMEM] * 5...  4.78 us
    unnamed x10, local copies, waits for them, and re-layouts  1.95 us
  transfers between devices with their start and end apart: 12, of which 11 were waited for; matrix products, arithmetic and copies ran while one was open for 0% of the time, Pallas kernels for 0%

profile of v2, /device:TPU:123, one launch (start us, length us, event | category | flops | bytes accessed | tf_op | source)
XLA Modules:
  0.0 66.9 jit_solution(1451925781173516785)
XLA Ops:
  0.0 0.0 copy-start.3
  0.0 0.9 %shard_map.64 = (f32[4,32,128]{2,1,0:T(8,128)S(1)}, f32[4,32,128]{2,1,0:T(8,128)S(1)}) custom-call(f32[4,128,128]{2,1,0:T(8,128)} %bitcast.4), custom_call_target="tpu_custom_call" | custom-call | tf_op jit(solution)/shard_map/pallas_call | solution.py:445
  0.9 2.1 %collective-permute-start = (f32[4,32,128]{2,1,0:T(8,128)S(1)}, f32[4,32,128]{2,1,0:T(8,128)S(1)}, u32[]{:S(2)}, u32[]{:S(2)}) collective-permute-start(f32[4,32,128]{2,1,0:T(8,128)S(1)} %get-tuple-element.25), channel_id=1, source_target_pairs={{0,16},{16,32},{32,48},{48,64},{64,80},{80,96},{96,112},{112,128},... | collective-permute-start | bytes 196616 | tf_op jit(solution)/shard_map/ppermute | solution.py:417
  3.1 0.0 copy-start
  3.1 0.0 collective-permute-start.1
  3.1 0.0 copy-done.3
  3.1 0.0 copy-start.1
  3.1 1.3 %copy-done.1 = bf16[4,2,256,256]{3,2,1,0:T(8,128)(2,1)S(1)} copy-done((bf16[4,2,256,256]{3,2,1,0:T(8,128)(2,1)S(1)}, bf16[4,2,256,256]{3,2,1,0:T(8,128)(2,1)}, u32[]{:S(2)}) %copy-start.1) | copy-done | bytes 1048600
  4.4 0.2 shard_map.65
  4.6 0.0 copy-start.2
  4.6 0.0 collective-permute-done.above_ref
  4.6 5.8 %collective-permute-done.1.below_ref = f32[4,32,128]{2,1,0:T(8,128)S(1)} collective-permute-done((f32[4,32,128]{2,1,0:T(8,128)S(1)}, f32[4,32,128]{2,1,0:T(8,128)S(1)}, u32[]{:S(2)}, u32[]{:S(2)}) %collective-permute-start.1) | collective-permute-done | bytes 65568 | tf_op jit(solution)/shard_map/ppermute | solution.py:417
  10.4 0.0 copy-done
  10.4 0.2 shard_map.66
  10.6 3.8 %collective-permute-start.2 = (f32[192,128]{1,0:T(8,128)S(1)}, f32[192,128]{1,0:T(8,128)S(1)}, u32[]{:S(2)}, u32[]{:S(2)}) collective-permute-start(f32[192,128]{1,0:T(8,128)S(1)} %get-tuple-element.28), channel_id=1, source_target_pairs={{0,1},{1,2},{2,3},{3,4},{4,5},{5,6},{6,7},{7,8},{8,9},{9,10},{10,1... | collective-permute-start | bytes 294920 | tf_op jit(solution)/shard_map/ppermute | solution.py:417
  14.4 0.0 collective-permute-start.3
  15.1 0.0 copy-start.4
  15.1 0.7 %copy-done.4 = s32[1,1,6,2]{2,3,1,0:T(2,128)S(1)} copy-done((s32[1,1,6,2]{2,3,1,0:T(2,128)S(1)}, s32[1,1,6,2]{2,3,1,0:T(2,128)}, u32[]{:S(2)}) %copy-start.4) | copy-done | bytes 72
  15.8 0.1 copy.7.offsets_ref
  15.8 0.0 copy-done.2
  15.8 0.1 shard_map.67.amplitude_ref
  16.0 0.1 collective-permute-done.2.from_left_ref
  16.1 3.9 %collective-permute-done.3.from_right_ref = f32[192,128]{1,0:T(8,128)S(1)} collective-permute-done((f32[192,128]{1,0:T(8,128)S(1)}, f32[192,128]{1,0:T(8,128)S(1)}, u32[]{:S(2)}, u32[]{:S(2)}) %collective-permute-start.3) | collective-permute-done | bytes 98336 | tf_op jit(solution)/shard_map/ppermute | solution.py:417
  20.0 4.8 %shard_map.68 = (f32[2,4,192,128]{3,2,1,0:T(8,128)S(1)}, f32[2,4,192,128]{3,2,1,0:T(8,128)S(1)}, f32[6,64,128]{2,1,0:T(8,128)S(1)}, f32[6,64,128]{2,1,0:T(8,128)S(1)}) custom-call(f32[4,128,128]{2,1,0:T(8,128)S(1)} %bitcast.6, f32[4,32,128]{2,1,0:T(8,128)S(1)} %collective-permute-done.above_ref, f32[4,32,128]{2,1,0:T(8,128)S(1)} %collective-permute-done.1.below_ref, ...), custom_call_target="tpu_custom_call" | custom-call | tf_op jit(solution)/shard_map/pallas_call | solution.py:473
  24.8 0.9 %collective-permute-start.4 = (f32[6,64,128]{2,1,0:T(8,128)S(1)}, f32[6,64,128]{2,1,0:T(8,128)S(1)}, u32[]{:S(2)}, u32[]{:S(2)}) collective-permute-start(f32[6,64,128]{2,1,0:T(8,128)S(1)} %get-tuple-element.33), channel_id=1, source_target_pairs={{0,16},{16,32},{32,48},{48,64},{64,80},{80,96},{96,112},{112,128},... | collective-permute-start | bytes 589832 | tf_op jit(solution)/shard_map/ppermute | solution.py:417
  25.7 0.0 collective-permute-start.5
  25.7 2.6 %collective-permute-done.4.from_up_ref = f32[6,64,128]{2,1,0:T(8,128)S(1)} collective-permute-done((f32[6,64,128]{2,1,0:T(8,128)S(1)}, f32[6,64,128]{2,1,0:T(8,128)S(1)}, u32[]{:S(2)}, u32[]{:S(2)}) %collective-permute-start.4) | collective-permute-done | bytes 196640 | tf_op jit(solution)/shard_map/ppermute | solution.py:417
  28.3 7.7 %collective-permute-done.5.from_down_ref = f32[6,64,128]{2,1,0:T(8,128)S(1)} collective-permute-done((f32[6,64,128]{2,1,0:T(8,128)S(1)}, f32[6,64,128]{2,1,0:T(8,128)S(1)}, u32[]{:S(2)}, u32[]{:S(2)}) %collective-permute-start.5) | collective-permute-done | bytes 196640 | tf_op jit(solution)/shard_map/ppermute | solution.py:417
  36.0 0.2 shard_map.69
  36.3 2.2 %collective-permute-start.6 = (f32[2,192,128]{2,1,0:T(8,128)S(1)}, f32[2,192,128]{2,1,0:T(8,128)S(1)}, u32[]{:S(2)}, u32[]{:S(2)}) collective-permute-start(f32[2,192,128]{2,1,0:T(8,128)S(1)} %get-tuple-element.36), channel_id=1, source_target_pairs={{0,1},{1,2},{2,3},{3,4},{4,5},{5,6},{6,7},{7,8},{8,9},{9,10},{10,1... | collective-permute-start | bytes 589832 | tf_op jit(solution)/shard_map/ppermute | solution.py:417
  38.5 0.0 collective-permute-start.7
  38.5 2.6 %collective-permute-done.6.from_left_ref = f32[2,192,128]{2,1,0:T(8,128)S(1)} collective-permute-done((f32[2,192,128]{2,1,0:T(8,128)S(1)}, f32[2,192,128]{2,1,0:T(8,128)S(1)}, u32[]{:S(2)}, u32[]{:S(2)}) %collective-permute-start.6) | collective-permute-done | bytes 196640 | tf_op jit(solution)/shard_map/ppermute | solution.py:417
  41.1 4.0 %collective-permute-done.7.from_right_ref = f32[2,192,128]{2,1,0:T(8,128)S(1)} collective-permute-done((f32[2,192,128]{2,1,0:T(8,128)S(1)}, f32[2,192,128]{2,1,0:T(8,128)S(1)}, u32[]{:S(2)}, u32[]{:S(2)}) %collective-permute-start.7) | collective-permute-done | bytes 196640 | tf_op jit(solution)/shard_map/ppermute | solution.py:417
  45.1 4.8 %shard_map.70 = (f32[4,128,128]{2,1,0:T(8,128)S(1)}, f32[2,4,192,128]{3,2,1,0:T(8,128)S(1)}, f32[6,32,128]{2,1,0:T(8,128)S(1)}, f32[6,32,128]{2,1,0:T(8,128)S(1)}) custom-call(f32[2,4,192,128]{3,2,1,0:T(8,128)S(1)} %get-tuple-element.31.b_ref, f32[2,4,192,128]{3,2,1,0:T(8,128)S(1)} %get-tuple-element.35.sum_ref, ...), custom_call_target="tpu_custom_call" | custom-call | tf_op jit(solution)/shard_map/pallas_call | solution.py:485
  49.9 0.7 %collective-permute-start.8 = (f32[6,32,128]{2,1,0:T(8,128)S(1)}, f32[6,32,128]{2,1,0:T(8,128)S(1)}, u32[]{:S(2)}, u32[]{:S(2)}) collective-permute-start(f32[6,32,128]{2,1,0:T(8,128)S(1)} %get-tuple-element.40), channel_id=1, source_target_pairs={{0,16},{16,32},{32,48},{48,64},{64,80},{80,96},{96,112},{112,128},... | collective-permute-start | bytes 294920 | tf_op jit(solution)/shard_map/ppermute | solution.py:417
  50.7 0.0 collective-permute-start.9
  50.7 1.6 %collective-permute-done.8.from_up_ref = f32[6,32,128]{2,1,0:T(8,128)S(1)} collective-permute-done((f32[6,32,128]{2,1,0:T(8,128)S(1)}, f32[6,32,128]{2,1,0:T(8,128)S(1)}, u32[]{:S(2)}, u32[]{:S(2)}) %collective-permute-start.8) | collective-permute-done | bytes 98336 | tf_op jit(solution)/shard_map/ppermute | solution.py:417
  52.3 6.0 %collective-permute-done.9.from_down_ref = f32[6,32,128]{2,1,0:T(8,128)S(1)} collective-permute-done((f32[6,32,128]{2,1,0:T(8,128)S(1)}, f32[6,32,128]{2,1,0:T(8,128)S(1)}, u32[]{:S(2)}, u32[]{:S(2)}) %collective-permute-start.9) | collective-permute-done | bytes 98336 | tf_op jit(solution)/shard_map/ppermute | solution.py:417
  58.3 0.2 shard_map.71
  58.5 2.2 %collective-permute-start.10 = (f32[128,128]{1,0:T(8,128)S(1)}, f32[128,128]{1,0:T(8,128)S(1)}, u32[]{:S(2)}, u32[]{:S(2)}) collective-permute-start(f32[128,128]{1,0:T(8,128)S(1)} %get-tuple-element.43), channel_id=1, source_target_pairs={{0,1},{1,2},{2,3},{3,4},{4,5},{5,6},{6,7},{7,8},{8,9},{9,10},{10,1... | collective-permute-start | bytes 196616 | tf_op jit(solution)/shard_map/ppermute | solution.py:417
  60.7 0.0 collective-permute-start.11
  60.7 1.3 %collective-permute-done.10.from_left_ref = f32[128,128]{1,0:T(8,128)S(1)} collective-permute-done((f32[128,128]{1,0:T(8,128)S(1)}, f32[128,128]{1,0:T(8,128)S(1)}, u32[]{:S(2)}, u32[]{:S(2)}) %collective-permute-start.10) | collective-permute-done | bytes 65568 | tf_op jit(solution)/shard_map/ppermute | solution.py:417
  62.0 3.9 %collective-permute-done.11.from_right_ref = f32[128,128]{1,0:T(8,128)S(1)} collective-permute-done((f32[128,128]{1,0:T(8,128)S(1)}, f32[128,128]{1,0:T(8,128)S(1)}, u32[]{:S(2)}, u32[]{:S(2)}) %collective-permute-start.11) | collective-permute-done | bytes 65568 | tf_op jit(solution)/shard_map/ppermute | solution.py:417
  65.9 0.8 %shard_map.72 = f32[4,128,128]{2,1,0:T(8,128)} custom-call(f32[4,128,128]{2,1,0:T(8,128)S(1)} %get-tuple-element.42.core_ref, f32[128,128]{1,0:T(8,128)S(1)} %collective-permute-done.10.from_left_ref, f32[128,128]{1,0:T(8,128)S(1)} %collective-permute-done.11.from_right_ref), custom_call_target="tpu_custom_call" | custom-call | tf_op jit(solution)/shard_map/pallas_call | solution.py:500
Async XLA Ops:
  0.0 3.1 %copy-start.3 = (f32[2,128,128]{2,1,0:T(8,128)S(1)}, f32[2,128,128]{2,1,0:T(8,128)}, u32[]{:S(2)}) copy-start(f32[2,128,128]{2,1,0:T(8,128)} %probe_hbm.1) | copy-start | bytes 393220
  0.9 3.7 %collective-permute-start = (f32[4,32,128]{2,1,0:T(8,128)S(1)}, f32[4,32,128]{2,1,0:T(8,128)S(1)}, u32[]{:S(2)}, u32[]{:S(2)}) collective-permute-start(f32[4,32,128]{2,1,0:T(8,128)S(1)} %get-tuple-element.25), channel_id=1, source_target_pairs={{0,16},{16,32},{32,48},{48,64},{64,80},{80,96},{96,112},{112,128},... | collective-permute-start | bytes 196616 | tf_op jit(solution)/shard_map/ppermute | solution.py:417
  3.1 7.3 %copy-start = (f32[2,2,128,128]{3,2,1,0:T(8,128)S(1)}, f32[2,2,128,128]{3,2,1,0:T(8,128)}, u32[]{:S(2)}) copy-start(f32[2,2,128,128]{3,2,1,0:T(8,128)} %param.6) | copy-start | bytes 786436
  3.1 7.3 %collective-permute-start.1 = (f32[4,32,128]{2,1,0:T(8,128)S(1)}, f32[4,32,128]{2,1,0:T(8,128)S(1)}, u32[]{:S(2)}, u32[]{:S(2)}) collective-permute-start(f32[4,32,128]{2,1,0:T(8,128)S(1)} %get-tuple-element.26), channel_id=1, source_target_pairs={{0,240},{16,0},{32,16},{48,32},{64,48},{80,64},{96,80},{112,96},{1... | collective-permute-start | bytes 196616 | tf_op jit(solution)/shard_map/ppermute | solution.py:417
  3.1 1.3 %copy-start.1 = (bf16[4,2,256,256]{3,2,1,0:T(8,128)(2,1)S(1)}, bf16[4,2,256,256]{3,2,1,0:T(8,128)(2,1)}, u32[]{:S(2)}) copy-start(bf16[4,2,256,256]{3,2,1,0:T(8,128)(2,1)} %constant.2.clone.w_hbm) | copy-start | bytes 3145732
  4.6 11.3 %copy-start.2 = (f32[1,1,6,128,128]{4,3,2,1,0:T(8,128)S(1)}, f32[1,1,6,128,128]{4,3,2,1,0:T(8,128)}, u32[]{:S(2)}) copy-start(f32[1,1,6,128,128]{4,3,2,1,0:T(8,128)} %param.8) | copy-start | bytes 1179652
  10.6 5.4 %collective-permute-start.2 = (f32[192,128]{1,0:T(8,128)S(1)}, f32[192,128]{1,0:T(8,128)S(1)}, u32[]{:S(2)}, u32[]{:S(2)}) collective-permute-start(f32[192,128]{1,0:T(8,128)S(1)} %get-tuple-element.28), channel_id=1, source_target_pairs={{0,1},{1,2},{2,3},{3,4},{4,5},{5,6},{6,7},{7,8},{8,9},{9,10},{10,1... | collective-permute-start | bytes 294920 | tf_op jit(solution)/shard_map/ppermute | solution.py:417
  14.4 5.6 %collective-permute-start.3 = (f32[192,128]{1,0:T(8,128)S(1)}, f32[192,128]{1,0:T(8,128)S(1)}, u32[]{:S(2)}, u32[]{:S(2)}) collective-permute-start(f32[192,128]{1,0:T(8,128)S(1)} %get-tuple-element.29.after_ref), channel_id=1, source_target_pairs={{0,15},{1,0},{2,1},{3,2},{4,3},{5,4},{6,5},{7,6},{8,7},{9,8},{10,9... | collective-permute-start | bytes 294920 | tf_op jit(solution)/shard_map/ppermute | solution.py:417
  15.1 0.7 %copy-start.4 = (s32[1,1,6,2]{2,3,1,0:T(2,128)S(1)}, s32[1,1,6,2]{2,3,1,0:T(2,128)}, u32[]{:S(2)}) copy-start(s32[1,1,6,2]{2,3,1,0:T(2,128)} %param.10) | copy-start | bytes 148
  24.8 3.5 %collective-permute-start.4 = (f32[6,64,128]{2,1,0:T(8,128)S(1)}, f32[6,64,128]{2,1,0:T(8,128)S(1)}, u32[]{:S(2)}, u32[]{:S(2)}) collective-permute-start(f32[6,64,128]{2,1,0:T(8,128)S(1)} %get-tuple-element.33), channel_id=1, source_target_pairs={{0,16},{16,32},{32,48},{48,64},{64,80},{80,96},{96,112},{112,128},... | collective-permute-start | bytes 589832 | tf_op jit(solution)/shard_map/ppermute | solution.py:417
  25.7 10.3 %collective-permute-start.5 = (f32[6,64,128]{2,1,0:T(8,128)S(1)}, f32[6,64,128]{2,1,0:T(8,128)S(1)}, u32[]{:S(2)}, u32[]{:S(2)}) collective-permute-start(f32[6,64,128]{2,1,0:T(8,128)S(1)} %get-tuple-element.34), channel_id=1, source_target_pairs={{0,240},{16,0},{32,16},{48,32},{64,48},{80,64},{96,80},{112,96},{1... | collective-permute-start | bytes 589832 | tf_op jit(solution)/shard_map/ppermute | solution.py:417
  36.3 4.8 %collective-permute-start.6 = (f32[2,192,128]{2,1,0:T(8,128)S(1)}, f32[2,192,128]{2,1,0:T(8,128)S(1)}, u32[]{:S(2)}, u32[]{:S(2)}) collective-permute-start(f32[2,192,128]{2,1,0:T(8,128)S(1)} %get-tuple-element.36), channel_id=1, source_target_pairs={{0,1},{1,2},{2,3},{3,4},{4,5},{5,6},{6,7},{7,8},{8,9},{9,10},{10,1... | collective-permute-start | bytes 589832 | tf_op jit(solution)/shard_map/ppermute | solution.py:417
  38.5 6.6 %collective-permute-start.7 = (f32[2,192,128]{2,1,0:T(8,128)S(1)}, f32[2,192,128]{2,1,0:T(8,128)S(1)}, u32[]{:S(2)}, u32[]{:S(2)}) collective-permute-start(f32[2,192,128]{2,1,0:T(8,128)S(1)} %get-tuple-element.37), channel_id=1, source_target_pairs={{0,15},{1,0},{2,1},{3,2},{4,3},{5,4},{6,5},{7,6},{8,7},{9,8},{10,9... | collective-permute-start | bytes 589832 | tf_op jit(solution)/shard_map/ppermute | solution.py:417
  49.9 2.4 %collective-permute-start.8 = (f32[6,32,128]{2,1,0:T(8,128)S(1)}, f32[6,32,128]{2,1,0:T(8,128)S(1)}, u32[]{:S(2)}, u32[]{:S(2)}) collective-permute-start(f32[6,32,128]{2,1,0:T(8,128)S(1)} %get-tuple-element.40), channel_id=1, source_target_pairs={{0,16},{16,32},{32,48},{48,64},{64,80},{80,96},{96,112},{112,128},... | collective-permute-start | bytes 294920 | tf_op jit(solution)/shard_map/ppermute | solution.py:417
  50.7 7.7 %collective-permute-start.9 = (f32[6,32,128]{2,1,0:T(8,128)S(1)}, f32[6,32,128]{2,1,0:T(8,128)S(1)}, u32[]{:S(2)}, u32[]{:S(2)}) collective-permute-start(f32[6,32,128]{2,1,0:T(8,128)S(1)} %get-tuple-element.41), channel_id=1, source_target_pairs={{0,240},{16,0},{32,16},{48,32},{64,48},{80,64},{96,80},{112,96},{1... | collective-permute-start | bytes 294920 | tf_op jit(solution)/shard_map/ppermute | solution.py:417
  58.5 3.5 %collective-permute-start.10 = (f32[128,128]{1,0:T(8,128)S(1)}, f32[128,128]{1,0:T(8,128)S(1)}, u32[]{:S(2)}, u32[]{:S(2)}) collective-permute-start(f32[128,128]{1,0:T(8,128)S(1)} %get-tuple-element.43), channel_id=1, source_target_pairs={{0,1},{1,2},{2,3},{3,4},{4,5},{5,6},{6,7},{7,8},{8,9},{9,10},{10,1... | collective-permute-start | bytes 196616 | tf_op jit(solution)/shard_map/ppermute | solution.py:417
  60.7 5.2 %collective-permute-start.11 = (f32[128,128]{1,0:T(8,128)S(1)}, f32[128,128]{1,0:T(8,128)S(1)}, u32[]{:S(2)}, u32[]{:S(2)}) collective-permute-start(f32[128,128]{1,0:T(8,128)S(1)} %get-tuple-element.44), channel_id=1, source_target_pairs={{0,15},{1,0},{2,1},{3,2},{4,3},{5,4},{6,5},{7,6},{8,7},{9,8},{10,9... | collective-permute-start | bytes 196616 | tf_op jit(solution)/shard_map/ppermute | solution.py:417

commit v3 on v2

--- a/solution.py
+++ b/solution.py
@@ -85,18 +85,13 @@
     return row > 0, row < rows - 1, col > 0, col < cols - 1
 
 
-def strips_kernel(core_hbm, top_ref, bottom_ref, sems):
-    size = core_hbm.shape[1]
-    copies = [
-        pltpu.make_async_copy(core_hbm.at[:, pl.ds(0, BORDER)], top_ref, sems.at[0]),
-        pltpu.make_async_copy(
-            core_hbm.at[:, pl.ds(size - BORDER, BORDER)], bottom_ref, sems.at[1]
-        ),
-    ]
-    for copy in copies:
-        copy.start()
-    for copy in copies:
-        copy.wait()
+def strips_kernel(core_hbm, left_ref, right_ref, core_ref, sem):
+    copy = pltpu.make_async_copy(core_hbm, core_ref, sem)
+    copy.start()
+    copy.wait()
+    planes = [core_ref[p] for p in range(4)]
+    left_ref[...] = pack_quarter(planes, 0)
+    right_ref[...] = pack_quarter(planes, 96)
 
 
 def stage_kernel(probe_hbm, w_hbm, probe_ref, w_ref, sems):
@@ -121,20 +116,22 @@
     lax.fori_loop(0, amplitude_ref.shape[0], root, 0)
 
 
-def halo_pack_kernel(core_ref, above_ref, below_ref, staged_ref, left_ref, right_ref):
+def halo_pack_kernel(core_ref, from_left_ref, from_right_ref, staged_ref, up_ref, down_ref):
     del staged_ref
-    has_up, has_down, _, _ = edges()
-    parts = (
-        (0, 32, above_ref, 0, has_up),
-        (32, 128, core_ref, 0, None),
-        (160, 32, below_ref, 0, has_down),
-    )
-    for start, length, ref, at, flag in parts:
-        planes = [ref[p, pl.ds(at, length), :] for p in range(4)]
-        if flag is not None:
-            planes = [jnp.where(flag, plane, 0.0) for plane in planes]
-        left_ref[pl.ds(start, length), :] = pack_quarter(planes, 0)
-        right_ref[pl.ds(start, length), :] = pack_quarter(planes, 96)
+    _, _, has_left, has_right = edges()
+    lane = lane_iota(BORDER)
+    for start, out_ref in ((0, up_ref), (core_ref.shape[1] - BORDER, down_ref)):
+        at = pl.ds(start, BORDER)
+        left = jnp.where(has_left, from_left_ref[at, :], 0.0)
+        right = jnp.where(has_right, from_right_ref[at, :], 0.0)
+        far = []
+        for p in range(4):
+            out_ref[p] = core_ref[p, at, :]
+            far.append(
+                outer(lane, unpack_quarter(right, p, 0), unpack_quarter(left, p, 96))
+            )
+        for p in range(2):
+            out_ref[4 + p] = pack_half(far[p], far[p + 2])
 
 
 def gradients(b_ref, probe_ref, amplitude_ref, live, offsets_ref, w_ref, g_ref, scratch):
@@ -278,17 +275,19 @@
     b_ref, g_ref, up_ref, down_ref, *scratch,
 ):
     has_up, has_down, has_left, has_right = edges()
-    rows = b_ref.shape[2]
-    lane = lane_iota(rows)
+    lane = lane_iota(core_ref.shape[1])
+    from_right = jnp.where(has_right, from_right_ref[...], 0.0)
+    from_left = jnp.where(has_left, from_left_ref[...], 0.0)
     for p in range(4):
-        b_ref[0, p, pl.ds(0, 32), :] = jnp.where(has_up, above_ref[p], 0.0)
         b_ref[0, p, pl.ds(32, 128), :] = core_ref[p]
-        b_ref[0, p, pl.ds(160, 32), :] = jnp.where(has_down, below_ref[p], 0.0)
-        from_right = jnp.where(has_right, from_right_ref[...], 0.0)
-        from_left = jnp.where(has_left, from_left_ref[...], 0.0)
-        b_ref[1, p] = outer(
+        b_ref[1, p, pl.ds(32, 128), :] = outer(
             lane, unpack_quarter(from_right, p, 0), unpack_quarter(from_left, p, 96)
         )
+        for t in range(2):
+            top = jnp.where(has_up, row_unpack(above_ref, t, p), 0.0)
+            bottom = jnp.where(has_down, row_unpack(below_ref, t, p), 0.0)
+            b_ref[t, p, pl.ds(0, 32), :] = top
+            b_ref[t, p, pl.ds(160, 32), :] = bottom
     gradients(
         b_ref, probe_ref, amplitude_ref, counts_ref[0, 0], offsets_ref, w_ref, g_ref, scratch
     )
@@ -442,14 +441,14 @@
     )
     full = (2, 4, tall, size)
 
-    top, bottom = call(
+    to_left, to_right, core = call(
         strips_kernel,
-        [(4, BORDER, size)] * 2,
+        [(size, LANES), (size, LANES), (4, size, size)],
         [HBM],
         4,
-        (pltpu.SemaphoreType.DMA((2,)),),
+        (pltpu.SemaphoreType.DMA(()),),
     )(pltpu.with_memory_space_constraint(core, pltpu.HBM))
-    above, below = exchange("row", top, bottom)
+    left, right = exchange("col", to_left, to_right)
     probe, weights = call(
         stage_kernel,
         [probe_field.shape, jax.ShapeDtypeStruct(weights.shape, weights.dtype)],
@@ -458,17 +457,17 @@
         (pltpu.SemaphoreType.DMA((2,)),),
         pl.CostEstimate(flops=0, bytes_accessed=2400000, transcendentals=0),
     )(probe_field, weights)
-    to_left, to_right = call(
-        halo_pack_kernel, [(tall, LANES)] * 2, [VMEM] * 3 + [ANY], 8
-    )(core, above, below, probe)
-    left, right = exchange("col", to_left, to_right)
+    up, down = call(
+        halo_pack_kernel, [(6, BORDER, size)] * 2, [VMEM] * 3 + [ANY], 8
+    )(core, left, right, probe)
+    above, below = exchange("row", up, down)
     (amplitude,) = call(
         amplitude_kernel,
         [own_intensity.shape],
         [VMEM, ANY],
         8,
         cost=pl.CostEstimate(flops=200000, bytes_accessed=800000, transcendentals=100000),
-    )(own_intensity, to_left)
+    )(own_intensity, up)
     common = (probe, amplitude, counts, own_offsets, weights)
     bordered, grads, up, down = call(
         first_kernel,

time: 67.1 us -> 66.8 us (level)
    unnamed x10 -> x8, local copies, waits for them, and re-layouts: 1.95 us -> 1.91 us
where the time goes in v3:
time: 66.8 us; the launch traced here: 66.6 us
  waiting for transfers between devices  39.7 us (59%)
  Pallas kernels  12.5 us (19%)
  starting transfers between devices  11.5 us (17%)
  local copies, waits for them, and re-layouts  2 us (3%)
  between operations  0.92 us (1%)
    ppermute x12, waiting for transfers between devices, shifted(): lax.ppermute(value, axis, [(i, (i + by) % count) for i in range(count)])  39.7 us
    ppermute x12, starting transfers between devices, shifted(): lax.ppermute(value, axis, [(i, (i + by) % count) for i in range(count)])  11.5 us
    pallas_call x1, Pallas kernels, local(): call(second_kernel, [(4, size, size), full, (6, 32, size), (6, 32, size)]...  4.82 us
    pallas_call x1, Pallas kernels, local(): call(first_kernel, [full, full, (6, 64, size), (6, 64, size)], [VMEM] * 5...  4.75 us
    unnamed x8, local copies, waits for them, and re-layouts  1.91 us
  transfers between devices with their start and end apart: 12, of which 11 were waited for; matrix products, arithmetic and copies ran while one was open for 0% of the time, Pallas kernels for 0%

profile of v3, /device:TPU:123, one launch (start us, length us, event | category | flops | bytes accessed | tf_op | source)
XLA Modules:
  0.0 66.6 jit_solution(7852689847588647890)
XLA Ops:
  0.0 0.0 copy-start.2
  0.0 1.2 %shard_map.64 = (f32[128,128]{1,0:T(8,128)S(1)}, f32[128,128]{1,0:T(8,128)S(1)}, f32[4,128,128]{2,1,0:T(8,128)S(1)}) custom-call(f32[4,128,128]{2,1,0:T(8,128)} %bitcast.5), custom_call_target="tpu_custom_call" | custom-call | tf_op jit(solution)/shard_map/pallas_call | solution.py:444
  1.2 2.9 %collective-permute-start = (f32[128,128]{1,0:T(8,128)S(1)}, f32[128,128]{1,0:T(8,128)S(1)}, u32[]{:S(2)}, u32[]{:S(2)}) collective-permute-start(f32[128,128]{1,0:T(8,128)S(1)} %get-tuple-element.27), channel_id=1, source_target_pairs={{0,1},{1,2},{2,3},{3,4},{4,5},{5,6},{6,7},{7,8},{8,9},{9,10},{10,1... | collective-permute-start | bytes 196616 | tf_op jit(solution)/shard_map/ppermute | solution.py:416
  4.1 0.0 collective-permute-start.1
  4.1 0.0 copy-done.2
  4.1 0.0 copy-start
  4.1 1.2 %copy-done = bf16[4,2,256,256]{3,2,1,0:T(8,128)(2,1)S(1)} copy-done((bf16[4,2,256,256]{3,2,1,0:T(8,128)(2,1)S(1)}, bf16[4,2,256,256]{3,2,1,0:T(8,128)(2,1)}, u32[]{:S(2)}) %copy-start) | copy-done | bytes 1048600
  5.3 0.2 shard_map.65
  5.5 0.0 copy-start.1
  5.5 0.0 collective-permute-done.from_left_ref
  5.6 3.7 %collective-permute-done.1.from_right_ref = f32[128,128]{1,0:T(8,128)S(1)} collective-permute-done((f32[128,128]{1,0:T(8,128)S(1)}, f32[128,128]{1,0:T(8,128)S(1)}, u32[]{:S(2)}, u32[]{:S(2)}) %collective-permute-start.1) | collective-permute-done | bytes 65568 | tf_op jit(solution)/shard_map/ppermute | solution.py:416
  9.3 0.2 shard_map.66
  9.5 3.9 %collective-permute-start.2 = (f32[6,32,128]{2,1,0:T(8,128)S(1)}, f32[6,32,128]{2,1,0:T(8,128)S(1)}, u32[]{:S(2)}, u32[]{:S(2)}) collective-permute-start(f32[6,32,128]{2,1,0:T(8,128)S(1)} %get-tuple-element.30), channel_id=1, source_target_pairs={{0,16},{16,32},{32,48},{48,64},{64,80},{80,96},{96,112},{112,128},... | collective-permute-start | bytes 294920 | tf_op jit(solution)/shard_map/ppermute | solution.py:416
  13.3 0.0 collective-permute-start.3
  14.0 0.0 copy-start.3
  14.0 0.7 %copy-done.3 = s32[1,1,6,2]{2,3,1,0:T(2,128)S(1)} copy-done((s32[1,1,6,2]{2,3,1,0:T(2,128)S(1)}, s32[1,1,6,2]{2,3,1,0:T(2,128)}, u32[]{:S(2)}) %copy-start.3) | copy-done | bytes 72
  14.7 0.1 copy.7.offsets_ref
  14.8 0.0 copy-done.1
  14.8 0.1 shard_map.67.amplitude_ref
  14.9 0.1 collective-permute-done.2.above_ref
  15.0 6.0 %collective-permute-done.3.below_ref = f32[6,32,128]{2,1,0:T(8,128)S(1)} collective-permute-done((f32[6,32,128]{2,1,0:T(8,128)S(1)}, f32[6,32,128]{2,1,0:T(8,128)S(1)}, u32[]{:S(2)}, u32[]{:S(2)}) %collective-permute-start.3) | collective-permute-done | bytes 98336 | tf_op jit(solution)/shard_map/ppermute | solution.py:416
  21.0 4.8 %shard_map.68 = (f32[2,4,192,128]{3,2,1,0:T(8,128)S(1)}, f32[2,4,192,128]{3,2,1,0:T(8,128)S(1)}, f32[6,64,128]{2,1,0:T(8,128)S(1)}, f32[6,64,128]{2,1,0:T(8,128)S(1)}) custom-call(f32[4,128,128]{2,1,0:T(8,128)S(1)} %get-tuple-element.26.core_ref, f32[6,32,128]{2,1,0:T(8,128)S(1)} %collective-permute-done.2.above_ref, ...), custom_call_target="tpu_custom_call" | custom-call | tf_op jit(solution)/shard_map/pallas_call | solution.py:472
  25.8 0.1 collective-permute-start.4
  25.8 0.5 collective-permute-start.5
  26.3 2.1 %collective-permute-done.4.from_up_ref = f32[6,64,128]{2,1,0:T(8,128)S(1)} collective-permute-done((f32[6,64,128]{2,1,0:T(8,128)S(1)}, f32[6,64,128]{2,1,0:T(8,128)S(1)}, u32[]{:S(2)}, u32[]{:S(2)}) %collective-permute-start.4) | collective-permute-done | bytes 196640 | tf_op jit(solution)/shard_map/ppermute | solution.py:416
  28.4 9.6 %collective-permute-done.5.from_down_ref = f32[6,64,128]{2,1,0:T(8,128)S(1)} collective-permute-done((f32[6,64,128]{2,1,0:T(8,128)S(1)}, f32[6,64,128]{2,1,0:T(8,128)S(1)}, u32[]{:S(2)}, u32[]{:S(2)}) %collective-permute-start.5) | collective-permute-done | bytes 196640 | tf_op jit(solution)/shard_map/ppermute | solution.py:416
  38.0 0.2 shard_map.69
  38.3 0.1 collective-permute-start.6
  38.4 1.5 %collective-permute-start.7 = (f32[2,192,128]{2,1,0:T(8,128)S(1)}, f32[2,192,128]{2,1,0:T(8,128)S(1)}, u32[]{:S(2)}, u32[]{:S(2)}) collective-permute-start(f32[2,192,128]{2,1,0:T(8,128)S(1)} %get-tuple-element.39), channel_id=1, source_target_pairs={{0,15},{1,0},{2,1},{3,2},{4,3},{5,4},{6,5},{7,6},{8,7},{9,8},{10,9... | collective-permute-start | bytes 589832 | tf_op jit(solution)/shard_map/ppermute | solution.py:416
  39.8 3.1 %collective-permute-done.6.from_left_ref = f32[2,192,128]{2,1,0:T(8,128)S(1)} collective-permute-done((f32[2,192,128]{2,1,0:T(8,128)S(1)}, f32[2,192,128]{2,1,0:T(8,128)S(1)}, u32[]{:S(2)}, u32[]{:S(2)}) %collective-permute-start.6) | collective-permute-done | bytes 196640 | tf_op jit(solution)/shard_map/ppermute | solution.py:416
  42.9 2.4 %collective-permute-done.7.from_right_ref = f32[2,192,128]{2,1,0:T(8,128)S(1)} collective-permute-done((f32[2,192,128]{2,1,0:T(8,128)S(1)}, f32[2,192,128]{2,1,0:T(8,128)S(1)}, u32[]{:S(2)}, u32[]{:S(2)}) %collective-permute-start.7) | collective-permute-done | bytes 196640 | tf_op jit(solution)/shard_map/ppermute | solution.py:416
  45.2 4.8 %shard_map.70 = (f32[4,128,128]{2,1,0:T(8,128)S(1)}, f32[2,4,192,128]{3,2,1,0:T(8,128)S(1)}, f32[6,32,128]{2,1,0:T(8,128)S(1)}, f32[6,32,128]{2,1,0:T(8,128)S(1)}) custom-call(f32[2,4,192,128]{3,2,1,0:T(8,128)S(1)} %get-tuple-element.33.b_ref, f32[2,4,192,128]{3,2,1,0:T(8,128)S(1)} %get-tuple-element.37.sum_ref, ...), custom_call_target="tpu_custom_call" | custom-call | tf_op jit(solution)/shard_map/pallas_call | solution.py:484
  50.1 1.1 %collective-permute-start.8 = (f32[6,32,128]{2,1,0:T(8,128)S(1)}, f32[6,32,128]{2,1,0:T(8,128)S(1)}, u32[]{:S(2)}, u32[]{:S(2)}) collective-permute-start(f32[6,32,128]{2,1,0:T(8,128)S(1)} %get-tuple-element.42), channel_id=1, source_target_pairs={{0,16},{16,32},{32,48},{48,64},{64,80},{80,96},{96,112},{112,128},... | collective-permute-start | bytes 294920 | tf_op jit(solution)/shard_map/ppermute | solution.py:416
  51.2 0.0 collective-permute-start.9
  51.2 1.6 %collective-permute-done.8.from_up_ref = f32[6,32,128]{2,1,0:T(8,128)S(1)} collective-permute-done((f32[6,32,128]{2,1,0:T(8,128)S(1)}, f32[6,32,128]{2,1,0:T(8,128)S(1)}, u32[]{:S(2)}, u32[]{:S(2)}) %collective-permute-start.8) | collective-permute-done | bytes 98336 | tf_op jit(solution)/shard_map/ppermute | solution.py:416
  52.8 6.0 %collective-permute-done.9.from_down_ref = f32[6,32,128]{2,1,0:T(8,128)S(1)} collective-permute-done((f32[6,32,128]{2,1,0:T(8,128)S(1)}, f32[6,32,128]{2,1,0:T(8,128)S(1)}, u32[]{:S(2)}, u32[]{:S(2)}) %collective-permute-start.9) | collective-permute-done | bytes 98336 | tf_op jit(solution)/shard_map/ppermute | solution.py:416
  58.8 0.2 shard_map.71
  59.0 1.4 %collective-permute-start.10 = (f32[128,128]{1,0:T(8,128)S(1)}, f32[128,128]{1,0:T(8,128)S(1)}, u32[]{:S(2)}, u32[]{:S(2)}) collective-permute-start(f32[128,128]{1,0:T(8,128)S(1)} %get-tuple-element.45), channel_id=1, source_target_pairs={{0,1},{1,2},{2,3},{3,4},{4,5},{5,6},{6,7},{7,8},{8,9},{9,10},{10,1... | collective-permute-start | bytes 196616 | tf_op jit(solution)/shard_map/ppermute | solution.py:416
  60.4 0.2 collective-permute-start.11
  60.6 1.6 %collective-permute-done.10.from_left_ref = f32[128,128]{1,0:T(8,128)S(1)} collective-permute-done((f32[128,128]{1,0:T(8,128)S(1)}, f32[128,128]{1,0:T(8,128)S(1)}, u32[]{:S(2)}, u32[]{:S(2)}) %collective-permute-start.10) | collective-permute-done | bytes 65568 | tf_op jit(solution)/shard_map/ppermute | solution.py:416
  62.2 3.4 %collective-permute-done.11.from_right_ref = f32[128,128]{1,0:T(8,128)S(1)} collective-permute-done((f32[128,128]{1,0:T(8,128)S(1)}, f32[128,128]{1,0:T(8,128)S(1)}, u32[]{:S(2)}, u32[]{:S(2)}) %collective-permute-start.11) | collective-permute-done | bytes 65568 | tf_op jit(solution)/shard_map/ppermute | solution.py:416
  65.6 0.8 %shard_map.72 = f32[4,128,128]{2,1,0:T(8,128)} custom-call(f32[4,128,128]{2,1,0:T(8,128)S(1)} %get-tuple-element.44.core_ref, f32[128,128]{1,0:T(8,128)S(1)} %collective-permute-done.10.from_left_ref, f32[128,128]{1,0:T(8,128)S(1)} %collective-permute-done.11.from_right_ref), custom_call_target="tpu_custom_call" | custom-call | tf_op jit(solution)/shard_map/pallas_call | solution.py:499
Async XLA Ops:
  0.0 4.1 %copy-start.2 = (f32[2,128,128]{2,1,0:T(8,128)S(1)}, f32[2,128,128]{2,1,0:T(8,128)}, u32[]{:S(2)}) copy-start(f32[2,128,128]{2,1,0:T(8,128)} %probe_hbm.1) | copy-start | bytes 393220
  1.2 4.4 %collective-permute-start = (f32[128,128]{1,0:T(8,128)S(1)}, f32[128,128]{1,0:T(8,128)S(1)}, u32[]{:S(2)}, u32[]{:S(2)}) collective-permute-start(f32[128,128]{1,0:T(8,128)S(1)} %get-tuple-element.27), channel_id=1, source_target_pairs={{0,1},{1,2},{2,3},{3,4},{4,5},{5,6},{6,7},{7,8},{8,9},{9,10},{10,1... | collective-permute-start | bytes 196616 | tf_op jit(solution)/shard_map/ppermute | solution.py:416
  4.1 5.2 %collective-permute-start.1 = (f32[128,128]{1,0:T(8,128)S(1)}, f32[128,128]{1,0:T(8,128)S(1)}, u32[]{:S(2)}, u32[]{:S(2)}) collective-permute-start(f32[128,128]{1,0:T(8,128)S(1)} %get-tuple-element.28), channel_id=1, source_target_pairs={{0,15},{1,0},{2,1},{3,2},{4,3},{5,4},{6,5},{7,6},{8,7},{9,8},{10,9... | collective-permute-start | bytes 196616 | tf_op jit(solution)/shard_map/ppermute | solution.py:416
  4.1 1.2 %copy-start = (bf16[4,2,256,256]{3,2,1,0:T(8,128)(2,1)S(1)}, bf16[4,2,256,256]{3,2,1,0:T(8,128)(2,1)}, u32[]{:S(2)}) copy-start(bf16[4,2,256,256]{3,2,1,0:T(8,128)(2,1)} %constant.2.clone.w_hbm) | copy-start | bytes 3145732
  5.5 9.2 %copy-start.1 = (f32[1,1,6,128,128]{4,3,2,1,0:T(8,128)S(1)}, f32[1,1,6,128,128]{4,3,2,1,0:T(8,128)}, u32[]{:S(2)}) copy-start(f32[1,1,6,128,128]{4,3,2,1,0:T(8,128)} %param.8) | copy-start | bytes 1179652
  9.5 5.5 %collective-permute-start.2 = (f32[6,32,128]{2,1,0:T(8,128)S(1)}, f32[6,32,128]{2,1,0:T(8,128)S(1)}, u32[]{:S(2)}, u32[]{:S(2)}) collective-permute-start(f32[6,32,128]{2,1,0:T(8,128)S(1)} %get-tuple-element.30), channel_id=1, source_target_pairs={{0,16},{16,32},{32,48},{48,64},{64,80},{80,96},{96,112},{112,128},... | collective-permute-start | bytes 294920 | tf_op jit(solution)/shard_map/ppermute | solution.py:416
  13.3 7.7 %collective-permute-start.3 = (f32[6,32,128]{2,1,0:T(8,128)S(1)}, f32[6,32,128]{2,1,0:T(8,128)S(1)}, u32[]{:S(2)}, u32[]{:S(2)}) collective-permute-start(f32[6,32,128]{2,1,0:T(8,128)S(1)} %get-tuple-element.31.after_ref), channel_id=1, source_target_pairs={{0,240},{16,0},{32,16},{48,32},{64,48},{80,64},{96,80},{112,96},{1... | collective-permute-start | bytes 294920 | tf_op jit(solution)/shard_map/ppermute | solution.py:416
  14.0 0.7 %copy-start.3 = (s32[1,1,6,2]{2,3,1,0:T(2,128)S(1)}, s32[1,1,6,2]{2,3,1,0:T(2,128)}, u32[]{:S(2)}) copy-start(s32[1,1,6,2]{2,3,1,0:T(2,128)} %param.10) | copy-start | bytes 148
  25.8 2.7 %collective-permute-start.4 = (f32[6,64,128]{2,1,0:T(8,128)S(1)}, f32[6,64,128]{2,1,0:T(8,128)S(1)}, u32[]{:S(2)}, u32[]{:S(2)}) collective-permute-start(f32[6,64,128]{2,1,0:T(8,128)S(1)} %get-tuple-element.35), channel_id=1, source_target_pairs={{0,16},{16,32},{32,48},{48,64},{64,80},{80,96},{96,112},{112,128},... | collective-permute-start | bytes 589832 | tf_op jit(solution)/shard_map/ppermute | solution.py:416
  25.8 12.2 %collective-permute-start.5 = (f32[6,64,128]{2,1,0:T(8,128)S(1)}, f32[6,64,128]{2,1,0:T(8,128)S(1)}, u32[]{:S(2)}, u32[]{:S(2)}) collective-permute-start(f32[6,64,128]{2,1,0:T(8,128)S(1)} %get-tuple-element.36), channel_id=1, source_target_pairs={{0,240},{16,0},{32,16},{48,32},{64,48},{80,64},{96,80},{112,96},{1... | collective-permute-start | bytes 589832 | tf_op jit(solution)/shard_map/ppermute | solution.py:416
  38.3 4.6 %collective-permute-start.6 = (f32[2,192,128]{2,1,0:T(8,128)S(1)}, f32[2,192,128]{2,1,0:T(8,128)S(1)}, u32[]{:S(2)}, u32[]{:S(2)}) collective-permute-start(f32[2,192,128]{2,1,0:T(8,128)S(1)} %get-tuple-element.38), channel_id=1, source_target_pairs={{0,1},{1,2},{2,3},{3,4},{4,5},{5,6},{6,7},{7,8},{8,9},{9,10},{10,1... | collective-permute-start | bytes 589832 | tf_op jit(solution)/shard_map/ppermute | solution.py:416
  38.4 6.9 %collective-permute-start.7 = (f32[2,192,128]{2,1,0:T(8,128)S(1)}, f32[2,192,128]{2,1,0:T(8,128)S(1)}, u32[]{:S(2)}, u32[]{:S(2)}) collective-permute-start(f32[2,192,128]{2,1,0:T(8,128)S(1)} %get-tuple-element.39), channel_id=1, source_target_pairs={{0,15},{1,0},{2,1},{3,2},{4,3},{5,4},{6,5},{7,6},{8,7},{9,8},{10,9... | collective-permute-start | bytes 589832 | tf_op jit(solution)/shard_map/ppermute | solution.py:416
  50.1 2.7 %collective-permute-start.8 = (f32[6,32,128]{2,1,0:T(8,128)S(1)}, f32[6,32,128]{2,1,0:T(8,128)S(1)}, u32[]{:S(2)}, u32[]{:S(2)}) collective-permute-start(f32[6,32,128]{2,1,0:T(8,128)S(1)} %get-tuple-element.42), channel_id=1, source_target_pairs={{0,16},{16,32},{32,48},{48,64},{64,80},{80,96},{96,112},{112,128},... | collective-permute-start | bytes 294920 | tf_op jit(solution)/shard_map/ppermute | solution.py:416
  51.2 7.7 %collective-permute-start.9 = (f32[6,32,128]{2,1,0:T(8,128)S(1)}, f32[6,32,128]{2,1,0:T(8,128)S(1)}, u32[]{:S(2)}, u32[]{:S(2)}) collective-permute-start(f32[6,32,128]{2,1,0:T(8,128)S(1)} %get-tuple-element.43), channel_id=1, source_target_pairs={{0,240},{16,0},{32,16},{48,32},{64,48},{80,64},{96,80},{112,96},{1... | collective-permute-start | bytes 294920 | tf_op jit(solution)/shard_map/ppermute | solution.py:416
  59.0 3.2 %collective-permute-start.10 = (f32[128,128]{1,0:T(8,128)S(1)}, f32[128,128]{1,0:T(8,128)S(1)}, u32[]{:S(2)}, u32[]{:S(2)}) collective-permute-start(f32[128,128]{1,0:T(8,128)S(1)} %get-tuple-element.45), channel_id=1, source_target_pairs={{0,1},{1,2},{2,3},{3,4},{4,5},{5,6},{6,7},{7,8},{8,9},{9,10},{10,1... | collective-permute-start | bytes 196616 | tf_op jit(solution)/shard_map/ppermute | solution.py:416
  60.4 5.2 %collective-permute-start.11 = (f32[128,128]{1,0:T(8,128)S(1)}, f32[128,128]{1,0:T(8,128)S(1)}, u32[]{:S(2)}, u32[]{:S(2)}) collective-permute-start(f32[128,128]{1,0:T(8,128)S(1)} %get-tuple-element.46), channel_id=1, source_target_pairs={{0,15},{1,0},{2,1},{3,2},{4,3},{5,4},{6,5},{7,6},{8,7},{9,8},{10,9... | collective-permute-start | bytes 196616 | tf_op jit(solution)/shard_map/ppermute | solution.py:416
